TPU v7x, 256 devices: a whole 4x4x8 slice. The times are simulated.
256 devices in a mesh: tok: 16 (over x_hi, y, core), ch: 16 (over z, x_lo).
Axes of the slice: x: 4 (x_hi: 2, x_lo: 2; x = x_hi * 2 + x_lo), y: 4, z: 8, core: 2. Of those that a mesh axis runs over, the one named last changes fastest.
Arguments:
- inputs: float32 [4096, 4096], P('tok', 'ch'), may hold values from -6 to 6
- grad_out: float32 [4096, 4096], P('tok', 'ch'), may hold values from -6 to 6
- blocks_one: float32 [16, 16, 4, 128, 128], P(None, 'ch'), may hold values from -0.1875 to 0.1875
- slots_one: int32 [16, 16, 4], P(None, 'ch'), may hold values from 0 to 128, as said below
- blocks_two: float32 [16, 16, 4, 128, 128], P(None, 'ch'), may hold values from -0.125 to 0.125
- slots_two: int32 [16, 16, 4], P(None, 'ch'), may hold values from 0 to 128, as said below
Outputs:
- grad_x: float32 [4096, 4096], P('tok', 'ch')
- grad_one: float32 [16, 16, 4, 128, 128], P('tok', 'ch')
- grad_two: float32 [16, 16, 4, 128, 128], P('tok', 'ch')
Inputs may be any that keep to these rules, and one draw needn't show every extreme that they name: For each hidden shard j, the live entries of slots_one[:, j, :] (those under 128) are distinct block positions; 128 marks an empty entry, live entries stand first in each owner's list, and in every shard one owner has all 4 entries live. Likewise for slots_two: distinct live positions in each shard, 128 marks an empty entry, live entries first, one owner of each shard with all 4 entries live.
All inputs are finite; a program needn't handle non-finite values.
Results may differ from a plain program's by a relative error of at most 0.0003.
Values sent between devices are 32-bit elements; how exact they have to be, the bound alone decides.
A program may use at most 192 MiB of HBM per device.

v0:
```python
import math

import jax
import jax.numpy as jnp
from jax import lax
from jax.sharding import PartitionSpec as P

H = 8192


HIGH = lax.Precision.HIGHEST
INNER = (((0,), (0,)), ((), ()))
OUTER = (((1,), (1,)), ((), ()))


def side_by_side(arrays, axis, dim, along):
    both = jnp.concatenate(arrays, axis=along)
    result, at, finished = (lax.all_gather(both, axis, axis=dim, tiled=True), 0, [])
    for a in arrays:
        finished.append(lax.slice_in_dim(result, at, at + a.shape[along], axis=along))
        at += a.shape[along]
    return tuple(finished)


def in_blocks(value, dim, peers):
    lengths = value.shape
    pieces = value.reshape(*lengths[:dim], peers, lengths[dim] // peers, *lengths[dim + 1 :])
    return jnp.moveaxis(pieces, dim, 0)


def summed_on_arrival(value, axis, dim):
    peers = lax.axis_size(axis)
    pieces = lax.all_to_all(in_blocks(value, dim, peers), axis, 0, 0, tiled=True)
    return jnp.sum(pieces, axis=0)


def side_by_side_2(arrays, axis, dim, along):
    both = jnp.concatenate(arrays, axis=along)
    result, at, finished = (lax.psum_scatter(both, axis, scatter_dimension=dim, tiled=True), 0, [])
    for a in arrays:
        finished.append(lax.slice_in_dim(result, at, at + a.shape[along], axis=along))
        at += a.shape[along]
    return tuple(finished)


def table_to_dense(block_table, first_dim, second_dim):
    block_size = block_table.shape[-1]
    grid = block_table.reshape(first_dim, second_dim, block_size, block_size).transpose(0, 2, 1, 3)
    return grid.reshape(first_dim * block_size, second_dim * block_size)


def dense_to_table(dense, first_dim, second_dim):
    block_size = dense.shape[0] // first_dim
    grid = dense.reshape(first_dim, block_size, second_dim, block_size).transpose(0, 2, 1, 3)
    return grid.reshape(first_dim * second_dim, block_size, block_size)


def rebuild(blocks, slot_ids, first_dim, second_dim):
    block_size = blocks.shape[-1]
    flat_blocks = blocks.reshape(-1, block_size, block_size)
    flat_ids = slot_ids.reshape(-1)
    empty = jnp.zeros((first_dim * second_dim, block_size, block_size), blocks.dtype)
    filled = empty.at[flat_ids].set(flat_blocks, mode="drop")
    return table_to_dense(filled, first_dim, second_dim)


def body(inputs, grad_out, blocks_one, slots_one, blocks_two, slots_two):
    owners = blocks_one.shape[0]
    entries = blocks_one.shape[2]
    block_size = blocks_one.shape[-1]
    x_full, dy_full = side_by_side((inputs, grad_out), "ch", 1, 0)
    features = x_full.shape[1]
    hidden = H // lax.axis_size("ch")
    feat_blocks = features // block_size
    hid_blocks = hidden // block_size
    dense_one = rebuild(blocks_one, slots_one, feat_blocks, hid_blocks)
    dense_two = rebuild(blocks_two, slots_two, hid_blocks, feat_blocks)
    pre_act = jnp.dot(x_full, dense_one, precision=HIGH)
    normal_cdf = 0.5 * (1.0 + lax.erf(pre_act * (1.0 / math.sqrt(2.0))))
    normal_pdf = jnp.exp(-0.5 * pre_act * pre_act) * (1.0 / math.sqrt(2.0 * math.pi))
    activated = pre_act * normal_cdf
    grad_act = lax.dot_general(dy_full, dense_two, OUTER, precision=HIGH)
    grad_pre = grad_act * (normal_cdf + pre_act * normal_pdf)
    grad_x = summed_on_arrival(
        lax.dot_general(dense_one, grad_pre, OUTER, precision=HIGH), "ch", 0
    ).T
    factor = 1.0 / math.sqrt(inputs.shape[0] * lax.axis_size("tok"))
    ids_one = slots_one.reshape(owners, entries)
    ids_two = slots_two.reshape(owners, entries)
    full_one = lax.dot_general(x_full, grad_pre, INNER, precision=HIGH)
    full_two = lax.dot_general(activated, dy_full, INNER, precision=HIGH)
    table_one = dense_to_table(full_one, feat_blocks, hid_blocks)
    table_two = dense_to_table(full_two, hid_blocks, feat_blocks)
    pack_one = jnp.take(table_one, ids_one, axis=0, mode="fill", fill_value=0.0)
    pack_two = jnp.take(table_two, ids_two, axis=0, mode="fill", fill_value=0.0)
    sum_one, sum_two = side_by_side_2((pack_one, pack_two), "tok", 0, 1)
    grad_one = sum_one * factor
    grad_two = sum_two * factor
    grad_one = grad_one.reshape(1, 1, entries, block_size, block_size)
    grad_two = grad_two.reshape(1, 1, entries, block_size, block_size)
    return (grad_x, grad_one, grad_two)


def solution(mesh):
    in_specs = (
        P("tok", "ch"),
        P("tok", "ch"),
        P(None, "ch", None, None, None),
        P(None, "ch", None),
        P(None, "ch", None, None, None),
        P(None, "ch", None),
    )
    out_specs = (P("tok", "ch"), P("tok", "ch", None, None, None), P("tok", "ch", None, None, None))
    return jax.shard_map(body, mesh=mesh, in_specs=in_specs, out_specs=out_specs, check_vma=False)
```

profile of v0, /device:TPU:1, one launch (start us, length us, event | category | flops | bytes accessed | tf_op | source)
XLA Modules:
  0.0 440.8 jit_solution(6348411282234933249)
XLA Ops:
  7.2 1.9 pad_maximum_fusion.1
  10.0 4.3 broadcast.43.clone
  14.3 11.8 %scatter_fusion = f32[128,128,128]{2,1,0:T(8,128)} fusion(f32[128,128,128]{2,1,0:T(8,128)} %broadcast.43.clone, s32[64]{0:T(128)S(1)} %fusion.29, f32[64,128,128]{2,1,0:T(8,128)} %bitcast.69), kind=kCustom, calls=%fused_computation.2 | custom fusion | bytes 12583168 | tf_op jit(solution)/shard_map/scatter | solution.py:63
  26.1 10.3 %copy.37 = f32[32,128,4,128]{1,0,3,2:T(8,128)} copy(f32[32,128,4,128]{3,1,2,0:T(8,128)} %bitcast.59) | data formatting | bytes 16777216 | tf_op jit(solution)/shard_map/transpose | solution.py:48
  36.6 4.3 broadcast.43.clone.1
  40.9 11.5 %scatter_fusion.1 = f32[128,128,128]{2,1,0:T(8,128)} fusion(f32[128,128,128]{2,1,0:T(8,128)} %broadcast.43.clone.1, s32[64]{0:T(128)S(1)} %fusion.30, f32[64,128,128]{2,1,0:T(8,128)} %bitcast.70), kind=kCustom, calls=%fused_computation.3 | custom fusion | bytes 12583168 | tf_op jit(solution)/shard_map/scatter | solution.py:63
  52.4 11.5 %copy.39 = f32[4,32,128,128]{3,1,2,0:T(8,128)} copy(f32[4,32,128,128]{3,2,1,0:T(8,128)} %bitcast.61) | data formatting | bytes 16777216 | tf_op jit(solution)/shard_map/reshape | solution.py:48
  64.5 131.4 %all-gather.2.cloned.1.call-done = f32[512,4096]{1,0:T(8,128)} async-done(((f32[512,256]{1,0:T(8,128)}), f32[512,4096]{1,0:T(8,128)}) %all-gather.2.cloned.1.call-update) | async-done | bytes 8388624 | tf_op jit(solution)/shard_map/all_gather | solution.py:18
  195.8 14.1 %fusion = f32[256,512]{1,0:T(8,128)S(1)} fusion(f32[64,8,32,128]{3,2,1,0:T(8,128)} %bitcast.62, f32[512,4096]{1,0:T(8,128)} %all-gather.2.cloned.1.call-done), kind=kOutput, calls=%fused_computation.4 | convolution fusion | flops 6442450944 | bytes 13107200 | tf_op jit(solution)/shard_map/dot_general | solution.py:78
  210.0 15.2 %fusion.15 = f32[256,512]{1,0:T(8,128)S(1)} fusion(f32[64,8,32,128]{3,2,1,0:T(8,128)} %bitcast.63, f32[512,4096]{1,0:T(8,128)S(1)} %copy-done, f32[256,512]{1,0:T(8,128)S(1)} %fusion), kind=kOutput, calls=%fused_computation.20 | convolution fusion | flops 6443630592 | bytes 13631488 | tf_op jit(solution)/shard_map/dot_general | solution.py:82
  225.2 9.7 %fusion.6 = f32[4096,512]{1,0:T(8,128)} fusion(f32[256,512]{1,0:T(8,128)S(1)} %fusion.15, f32[512,4096]{1,0:T(8,128)S(1)} %copy-done), kind=kOutput, calls=%fused_computation.11 | convolution fusion | flops 6442450944 | bytes 13107200 | tf_op jit(solution)/shard_map/dot_general | solution.py:90
  234.8 9.9 %reshape.126 = f32[32,128,4,128]{3,2,1,0:T(4,128)} reshape(f32[4096,512]{1,0:T(8,128)} %fusion.6) | data formatting | bytes 16777216 | tf_op jit(solution)/shard_map/reshape | solution.py:54
  244.7 7.9 %copy.43 = f32[32,128,4,128]{3,1,2,0:T(8,128)} copy(f32[32,128,4,128]{3,2,1,0:T(4,128)} %reshape.126) | data formatting | bytes 16777216 | tf_op jit(solution)/shard_map/reshape | solution.py:54
  252.6 9.5 %fusion.12 = f32[64,8,32,128]{3,1,2,0:T(8,128)S(1)} fusion(f32[512,4096]{1,0:T(8,128)} %all-gather.2.cloned.1.call-done, f32[256,512]{1,0:T(8,128)S(1)} %fusion), kind=kOutput, calls=%fused_computation.17 | convolution fusion | flops 6442975232 | bytes 13107200 | tf_op jit(solution)/shard_map/dot_general | solution.py:91
  264.0 8.1 %copy.46 = f32[4,128,32,128]{3,1,2,0:T(8,128)} copy(f32[4,128,32,128]{3,2,1,0:T(8,128)S(1)} %bitcast.64) | data formatting | bytes 16777216 | tf_op jit(solution)/shard_map/reshape | solution.py:54
  272.1 6.1 %gather_fusion = f32[64,128,128]{2,1,0:T(8,128)} fusion(f32[128,128,128]{2,1,0:T(8,128)} %bitcast.65, s32[1024]{0:T(1024)S(1)} %pad_clamp_fusion.1), kind=kCustom, calls=%fused_computation.clone | custom fusion | bytes 8388864 | tf_op jit(solution)/shard_map/jit(_take)/gather | solution.py:94
  278.2 6.2 %gather_fusion.1 = f32[64,128,128]{2,1,0:T(8,128)} fusion(f32[128,128,128]{2,1,0:T(8,128)} %bitcast.66, s32[1024]{0:T(1024)S(1)} %pad_clamp_fusion), kind=kCustom, calls=%fused_computation.1.clone | custom fusion | bytes 8388864 | tf_op jit(solution)/shard_map/jit(_take)/gather | solution.py:95
  284.3 4.1 broadcast_select_fusion
  288.4 3.8 pad_maximum_fusion
  292.3 14.2 %copy.49 = f32[32,128,4,128]{3,2,1,0:T(4,128)} copy(f32[32,128,4,128]{3,1,2,0:T(8,128)} %bitcast.60) | data formatting | bytes 16777216 | tf_op jit(solution)/shard_map/dot_general | solution.py:85
  306.4 10.7 %reshape.179 = f32[16,256,512]{2,1,0:T(8,128)} reshape(f32[32,128,4,128]{3,2,1,0:T(4,128)} %copy.49) | data formatting | bytes 16777216 | tf_op jit(solution)/shard_map/dot_general | solution.py:85
  317.1 9.6 %fusion.24 = f32[16,256,256]{2,1,0:T(8,128)S(1)} fusion(f32[16,256,512]{2,1,0:T(8,128)} %reshape.179, f32[256,512]{1,0:T(8,128)S(1)} %fusion.15), kind=kOutput, calls=%fused_computation.27 | convolution fusion | flops 6442450944 | bytes 13107200 | tf_op jit(solution)/shard_map/dot_general | solution.py:85
  326.8 101.5 %all_to_all.5 = f32[16,256,256]{2,1,0:T(8,128)} all-to-all(f32[16,256,256]{2,1,0:T(8,128)S(1)} %fusion.24), channel_id=1, replica_groups=mesh['tok'=16,'ch'=16] {'ch'}, dimensions={0} | all-to-all | bytes 8388608 | tf_op jit(solution)/shard_map/all_to_all | solution.py:33
  428.3 2.5 reduce_sum.9
  (32 shorter events, 6.3 us)
Async XLA Ops:
  7.2 188.7 %all-gather.2.cloned.1.call-start = ((), (), s32[]{:S(2)}) async-start(), calls=%async_computation.2 | async-start | bytes 8912896 | tf_op jit(solution)/shard_map/all_gather | solution.py:18
  9.1 422.6 %reduce-scatter.2.cloned.1.call-start = ((), (), s32[]{:S(2)}) async-start(), calls=%async_computation.3 | async-start | bytes 8912896 | tf_op jit(solution)/shard_map/reduce_scatter | solution.py:39
  26.1 10.3 %copy-start.2 = (s32[16,1,4]{0,2,1:T(4,128)S(1)}, s32[16,1,4]{0,2,1:T(4,128)}, u32[]{:S(2)}) copy-start(s32[16,1,4]{0,2,1:T(4,128)} %param.13) | copy-start | bytes 772
  52.4 11.5 %copy-start.1 = (s32[16,1,4]{0,2,1:T(4,128)S(1)}, s32[16,1,4]{0,2,1:T(4,128)}, u32[]{:S(2)}) copy-start(s32[16,1,4]{0,2,1:T(4,128)} %param.11) | copy-start | bytes 772
  195.8 14.1 %copy-start = (f32[512,4096]{1,0:T(8,128)S(1)}, f32[512,4096]{1,0:T(8,128)}, u32[]{:S(2)}) copy-start(f32[512,4096]{1,0:T(8,128)} %all-gather.2.cloned.1.call-done) | copy-start | bytes 25165828
Sparse Core Ops, SparseCore 0:
  9.8 186.0 all-gather.1
  292.4 139.1 reduce-scatter.1
where the time goes:
time: 449 us; the launch traced here: 441 us
  waiting for transfers between devices  131 us (29%)
  local copies, waits for them, and re-layouts  121 us (27%)
  blocking collectives  102 us (23%)
  matrix products  58.1 us (13%)
  between operations  14.6 us (3%)
  other arithmetic  14.2 us (3%)
    all_gather x1, waiting for transfers between devices, side_by_side(): lax.all_gather(both, axis, axis=dim, tiled=True)  131 us
    all_to_all x1, blocking collectives, summed_on_arrival(): lax.all_to_all(in_blocks(value, dim, peers), axis, 0, 0, tiled=True)  102 us
    reshape x3, local copies, waits for them, and re-layouts, dense_to_table(): dense.reshape(first_dim, block_size, second_dim, block_size)  25.8 us
    dot_general x2, local copies, waits for them, and re-layouts, body(): lax.dot_general(dense_one, grad_pre, OUTER, precision=HIGH)  24.9 us
    scatter x2, local copies, waits for them, and re-layouts, rebuild(): filled = empty.at[flat_ids].set(flat_blocks, mode='drop')  23.3 us
    dot_general x1, matrix products, body(): grad_act = lax.dot_general(dy_full, dense_two, OUTER, precision=HIGH)  15.2 us
    dot_general x1, matrix products, body(): pre_act = jnp.dot(x_full, dense_one, precision=HIGH)  14.1 us
    reshape x1, local copies, waits for them, and re-layouts, table_to_dense(): block_table.reshape(first_dim, second_dim, block_size, block_size)  11.5 us
  transfers between devices with their start and end apart: 2, of which 1 were waited for; matrix products, arithmetic and copies ran while one was open for 21% of the time, Pallas kernels for 0%

commit v1 on v0

v1 whole, which is shorter than its diff:
```python
import functools
import math

import jax
import jax.numpy as jnp
from jax import lax
from jax.experimental import pallas as pl
from jax.experimental.pallas import tpu as pltpu
from jax.sharding import PartitionSpec as P

F32 = jnp.float32
BF16 = jnp.bfloat16
MESH = pl.DeviceIdType.MESH
NZ, NXL, NXH, NY = 8, 2, 2, 4

SLOTS = [
    (0, 0),
    (0, -1), (0, 1), (1, 0),
    (0, -2), (0, 2), (1, 1),
    (0, -3), (0, 3), (1, -1),
    (0, 4), (1, -2), (1, 2),
    (1, -3), (1, 3), (1, 4),
]
SLOT = {key: at for at, key in enumerate(SLOTS)}
SLOT[(0, -4)] = SLOT[(0, 4)]
SLOT[(1, -4)] = SLOT[(1, 4)]
NT = (((1,), (1,)), ((), ()))
NN = (((1,), (0,)), ((), ()))

N_COPIES = 60 + 17 + 22


def dot(a, b, dims):
    return lax.dot_general(a, b, dims, preferred_element_type=F32)


def split(v):
    high = v.astype(BF16)
    return high, (v - high.astype(F32)).astype(BF16)


def kernel(
    tab, x_in, dy_in, w1_hbm, w2_hbm,
    gx_out, g1_out, g2_out,
    raw1, raw2, xg, dyg, w1h, w1l, w2h, w2l, table,
    sh, sl, pre, ga, slope, act_th, act_tl, gp_th, gp_tl, gph, gpl,
    gx, rs_buf, core_buf, y_buf, far_buf,
    send_sem, recv_sem, local_sem,
):
    t = lax.axis_index("tok")
    c = lax.axis_index("ch")
    core = lax.rem(t, 2)
    y = lax.rem(lax.div(t, 2), NY)
    xh = lax.div(t, 2 * NY)
    xl = lax.rem(c, 2)
    z = lax.div(c, 2)

    def at_z(step):
        return (t, lax.rem(z + step, NZ) * 2 + xl)

    def at_y(step):
        return ((xh * NY + lax.rem(y + step, NY)) * 2 + core, c)

    zp, zm = at_z(1), at_z(NZ - 1)
    yp, ym = at_y(1), at_y(NY - 1)
    xp = (t, z * 2 + (1 - xl))
    cp = ((xh * NY + y) * 2 + (1 - core), c)
    hp = (((1 - xh) * NY + y) * 2 + core, c)

    fetch1 = pltpu.make_async_copy(w1_hbm, raw1.at[pl.ds(0, 64)], local_sem.at[0])
    fetch2 = pltpu.make_async_copy(w2_hbm, raw2.at[pl.ds(0, 64)], local_sem.at[1])
    fetch1.start()
    fetch2.start()

    barrier = pltpu.get_barrier_semaphore()
    for peer in (zp, zm, xp, yp, ym, cp, hp):
        pl.semaphore_signal(barrier, inc=1, device_id=peer, device_id_type=MESH)
    pl.semaphore_wait(barrier, 7)

    copies = []

    def send(src, dst, peer):
        at = len(copies)
        copy = pltpu.make_async_remote_copy(
            src_ref=src, dst_ref=dst, send_sem=send_sem.at[at], recv_sem=recv_sem.at[at],
            device_id=peer, device_id_type=MESH,
        )
        copy.start()
        copies.append(copy)
        return copy

    rows = {"a": pl.ds(0, 128), "b": pl.ds(128, 128)}
    arrivals = {}

    def forward(phase, source, col, dz, half, link):
        peer = {"+": zp, "-": zm, "x": xp}[link]
        to = {"+": (col, dz - 1), "-": (col, dz + 1), "x": (1 - col, dz)}[link]
        buf = xg if phase == 0 else dyg
        src = source if (col, dz) == (0, 0) else buf.at[SLOT[(col, dz)]]
        copy = send(src.at[rows[half]], buf.at[SLOT[to], rows[half]], peer)
        arrivals[(phase, SLOT[to], half)] = copy

    def arrive(phase, key, halves="ab"):
        for half in halves:
            arrivals[(phase, SLOT[key], half)].wait_recv()

    def open_phase(phase, source):
        for half in "ab":
            for link in "+-x":
                forward(phase, source, 0, 0, half, link)

    def round_1(phase, source):
        for half in "ab":
            arrive(phase, (0, -1), half)
            forward(phase, source, 0, -1, half, "+")
            arrive(phase, (0, 1), half)
            forward(phase, source, 0, 1, half, "-")
            forward(phase, source, 0, 1, half, "x")
        for half in "ab":
            forward(phase, source, 0, -1, half, "x")
        arrive(phase, (1, 0))

    def round_2(phase, source):
        for half in "ab":
            arrive(phase, (0, -2), half)
            forward(phase, source, 0, -2, half, "+")
            arrive(phase, (0, 2), half)
            forward(phase, source, 0, 2, half, "-")
        arrive(phase, (1, 1))

    def round_3(phase, source):
        arrive(phase, (0, -3), "a")
        forward(phase, source, 0, -3, "a", "+")
        forward(phase, source, 0, -3, "a", "x")
        for half in "ab":
            forward(phase, source, 1, 1, half, "-")
        arrive(phase, (0, 3), "a")
        arrive(phase, (0, 3), "b")
        forward(phase, source, 0, 3, "b", "-")
        forward(phase, source, 0, 3, "b", "x")
        arrive(phase, (0, -3), "b")
        arrive(phase, (1, -1))
        for half in "ab":
            forward(phase, source, 1, -1, half, "+")
        forward(phase, source, 0, -3, "b", "x")
        forward(phase, source, 0, 3, "a", "x")

    def round_4(phase, source):
        arrive(phase, (0, 4))
        arrive(phase, (1, -3), "a")
        forward(phase, source, 1, -3, "a", "+")
        arrive(phase, (1, 3), "b")
        forward(phase, source, 1, 3, "b", "-")

    def round_5(phase):
        arrive(phase, (1, -2))
        arrive(phase, (1, 2))
        arrive(phase, (1, -3), "b")
        arrive(phase, (1, 3), "a")
        arrive(phase, (1, 4))

    def take_x(s, carry):
        for q in range(2):
            for h in range(4):
                high, low = split(raw1[tab[s * 8 + q * 4 + h]])
                w1h[s, pl.ds(q * 128, 128), pl.ds(h * 128, 128)] = high
                w1l[s, pl.ds(q * 128, 128), pl.ds(h * 128, 128)] = low
        high, low = split(xg[s])
        sh[...] = high
        sl[...] = low
        pre[...] += (
            dot(sh[...], w1h[s], NN) + dot(sh[...], w1l[s], NN) + dot(sl[...], w1h[s], NN)
        )
        return carry

    def to_table(s, th, tl):
        full = dot(th[...], sh[...], NN) + dot(th[...], sl[...], NN) + dot(tl[...], sh[...], NN)
        for q in range(2):
            for h in range(4):
                table[s * 8 + q * 4 + h] = full[h * 128 : h * 128 + 128, q * 128 : q * 128 + 128]

    def take_dy(s, carry):
        for q in range(2):
            for h in range(4):
                high, low = split(raw2[tab[128 + s * 8 + q * 4 + h]])
                w2h[pl.ds(h * 128, 128), pl.ds(q * 128, 128)] = high
                w2l[pl.ds(h * 128, 128), pl.ds(q * 128, 128)] = low
        high, low = split(dyg[s])
        sh[...] = high
        sl[...] = low
        ga[...] += (
            dot(sh[...], w2h[...], NT) + dot(sh[...], w2l[...], NT) + dot(sl[...], w2h[...], NT)
        )
        to_table(s, act_th, act_tl)
        return carry

    def take_w1(s, carry):
        high, low = split(xg[s])
        sh[...] = high
        sl[...] = low
        to_table(s, gp_th, gp_tl)
        return carry

    def grad_x(s, carry):
        gx[s] = dot(gph[...], w1h[s], NT) + dot(gph[...], w1l[s], NT) + dot(gpl[...], w1h[s], NT)
        return carry

    def run(body, first, last):
        lax.fori_loop(first, last, body, 0)

    def transposed(value, r, th, tl):
        high, low = split(value.T)
        th[:, r] = high
        tl[:, r] = low

    open_phase(0, x_in)
    xg[0] = x_in[...]
    pre[...] = jnp.zeros_like(pre)
    raw1[64] = jnp.zeros((128, 128), F32)
    fetch1.wait()
    run(take_x, 0, 1)
    round_1(0, x_in)
    run(take_x, 1, 4)
    round_2(0, x_in)
    run(take_x, 4, 7)
    round_3(0, x_in)
    run(take_x, 7, 10)
    dyg[0] = dy_in[...]
    ga[...] = jnp.zeros_like(ga)
    raw2[64] = jnp.zeros((128, 128), F32)
    table[128] = jnp.zeros((128, 128), F32)
    fetch2.wait()
    round_4(0, x_in)
    open_phase(1, dy_in)
    run(take_x, 10, 11)
    round_5(0)
    run(take_x, 11, 16)
    round_1(1, dy_in)
    for part in range(2):
        r = pl.ds(part * 128, 128)
        p = pre[r, :]
        cdf = 0.5 * (1.0 + lax.erf(p * (1.0 / math.sqrt(2.0))))
        pdf = jnp.exp(-0.5 * p * p) * (1.0 / math.sqrt(2.0 * math.pi))
        slope[r, :] = cdf + p * pdf
        transposed(p * cdf, r, act_th, act_tl)
    run(take_dy, 0, 4)
    round_2(1, dy_in)
    run(take_dy, 4, 7)
    round_3(1, dy_in)
    run(take_dy, 7, 10)
    round_4(1, dy_in)
    run(take_dy, 10, 11)
    round_5(1)
    run(take_dy, 11, 16)

    def pack(raw, offset, rxh):
        def one(i, carry):
            rc = lax.div(i, NY)
            ry = lax.rem(i, NY)
            owner_y = lax.rem(y + ry, NY)
            owner_x = xh + rxh - 2 * xh * rxh
            owner_c = core + rc - 2 * core * rc
            owner = (owner_x * NY + owner_y) * 2 + owner_c
            for e in range(4):
                raw[((rc * 2 + rxh) * NY + ry) * 4 + e] = table[tab[offset + owner * 4 + e]]
            return carry

        lax.fori_loop(0, 2 * NY, one, 0)

    def mine(raw, rxh, ry, first, count):
        return raw.at[pl.ds((rxh * NY + ry) * 4 + first, count)]

    def swap_cores(w, raw, rxh):
        return send(raw.at[pl.ds((2 + rxh) * 16, 16)], core_buf.at[w, rxh], cp)

    def add_core(copy, w, raw, rxh):
        copy.wait_recv()
        raw[pl.ds(rxh * 16, 16)] = raw[pl.ds(rxh * 16, 16)] + core_buf[w, rxh]

    def y_far(w, raw, rxh):
        return (
            send(mine(raw, rxh, 2, 0, 2), y_buf.at[w, rxh, 0, pl.ds(0, 2)], yp),
            send(mine(raw, rxh, 2, 2, 2), y_buf.at[w, rxh, 1, pl.ds(0, 2)], ym),
        )

    def y_near(pair, w, raw, rxh):
        at = (rxh * NY + 1) * 4
        pair[0].wait_recv()
        raw[pl.ds(at, 2)] = raw[pl.ds(at, 2)] + y_buf[w, rxh, 0, pl.ds(0, 2)]
        one = send(mine(raw, rxh, 1, 0, 4), y_buf.at[w, rxh, 0, pl.ds(2, 4)], yp)
        at = (rxh * NY + 3) * 4 + 2
        pair[1].wait_recv()
        raw[pl.ds(at, 2)] = raw[pl.ds(at, 2)] + y_buf[w, rxh, 1, pl.ds(0, 2)]
        two = send(mine(raw, rxh, 3, 0, 4), y_buf.at[w, rxh, 1, pl.ds(2, 4)], ym)
        return one, two

    def y_home(pair, w, raw, rxh):
        at = rxh * NY * 4
        pair[0].wait_recv()
        pair[1].wait_recv()
        raw[pl.ds(at, 4)] = (
            raw[pl.ds(at, 4)] + y_buf[w, rxh, 0, pl.ds(2, 4)] + y_buf[w, rxh, 1, pl.ds(2, 4)]
        )

    def far(w, raw):
        return send(mine(raw, 1, 0, 0, 4), far_buf.at[w], hp)

    def rs_send(col, dz, half, link):
        peer = {"+": zp, "-": zm, "x": xp}[link]
        to = {"+": (col, dz - 1), "-": (col, dz + 1), "x": (1 - col, dz)}[link]
        r = rows[half] if half else pl.ds(0, 256)
        index = len(rs_slots)
        copy = send(gx.at[SLOT[(col, dz)], r], rs_buf.at[index, r], peer)
        rs_slots.append((copy, index, SLOT[to], r))
        return index

    rs_slots = []

    def rs_add(index):
        copy, at, slot, r = rs_slots[index]
        copy.wait_recv()
        gx[slot, r] = gx[slot, r] + rs_buf[at, r]

    pack(raw2, 256 + 64, 1)
    core_21 = swap_cores(1, raw2, 1)
    pack(raw2, 256 + 64, 0)
    core_20 = swap_cores(1, raw2, 0)

    for part in range(2):
        r = pl.ds(part * 128, 128)
        grad_pre = ga[r, :] * slope[r, :]
        high, low = split(grad_pre)
        gph[r, :] = high
        gpl[r, :] = low
        transposed(grad_pre, r, gp_th, gp_tl)

    run(grad_x, 15, 16)
    p4a = rs_send(1, 4, "a", "+")
    p4b = rs_send(1, -4, "b", "-")
    run(grad_x, 10, 15)
    o4a = rs_send(0, 4, "a", "+")
    o4b = rs_send(0, -4, "b", "-")

    add_core(core_21, 1, raw2, 1)
    far_21 = y_far(1, raw2, 1)
    add_core(core_20, 1, raw2, 0)
    far_20 = y_far(1, raw2, 0)

    run(grad_x, 0, 10)
    p0 = rs_send(1, 0, None, "x")
    rs_add(p4a)
    p3a = rs_send(1, 3, None, "+")
    rs_add(p4b)
    p3b = rs_send(1, -3, None, "-")
    rs_add(o4a)
    o3a = rs_send(0, 3, None, "+")
    rs_add(o4b)
    o3b = rs_send(0, -3, None, "-")

    run(take_w1, 0, 8)
    near_21 = y_near(far_21, 1, raw2, 1)
    near_20 = y_near(far_20, 1, raw2, 0)
    run(take_w1, 8, 16)
    pack(raw1, 256, 1)
    core_11 = swap_cores(0, raw1, 1)
    pack(raw1, 256, 0)
    core_10 = swap_cores(0, raw1, 0)

    rs_add(p3a)
    p2a = rs_send(1, 2, None, "+")
    rs_add(p3b)
    p2b = rs_send(1, -2, None, "-")
    add_core(core_11, 0, raw1, 1)
    far_11 = y_far(0, raw1, 1)
    add_core(core_10, 0, raw1, 0)
    far_10 = y_far(0, raw1, 0)
    rs_add(p0)
    rs_add(o3a)
    o2a = rs_send(0, 2, None, "+")
    rs_add(o3b)
    o2b = rs_send(0, -2, None, "-")
    y_home(near_21, 1, raw2, 1)
    far_2 = far(1, raw2)
    rs_add(p2a)
    p1a = rs_send(1, 1, None, "x")
    rs_add(p2b)
    p1b = rs_send(1, -1, None, "x")
    near_11 = y_near(far_11, 0, raw1, 1)
    y_home(near_20, 1, raw2, 0)
    near_10 = y_near(far_10, 0, raw1, 0)
    rs_add(o2a)
    rs_add(p1a)
    o1a = rs_send(0, 1, None, "+")
    rs_add(o2b)
    rs_add(p1b)
    o1b = rs_send(0, -1, None, "-")
    y_home(near_11, 0, raw1, 1)
    far_1 = far(0, raw1)
    far_2.wait_recv()
    g2_out[...] = raw2[pl.ds(0, 4)] + far_buf[1]
    rs_add(o1a)
    rs_add(o1b)
    gx_out[...] = gx[0]
    y_home(near_10, 0, raw1, 0)
    far_1.wait_recv()
    g1_out[...] = raw1[pl.ds(0, 4)] + far_buf[0]
    for copy in copies:
        copy.wait_send()
    assert len(copies) == N_COPIES


def index_tables(slots_one, slots_two):
    c = lax.axis_index("ch")
    z, xl = c // 2, c % 2
    held = jnp.array([dz % NZ for _, dz in SLOTS], jnp.int32)
    other = jnp.array([col for col, _ in SLOTS], jnp.int32)
    shard = ((z + held) % NZ) * 2 + jnp.where(other == 1, 1 - xl, xl)
    place = jnp.arange(128, dtype=jnp.int32)
    q, h = (place // 4) % 2, place % 4
    f = jnp.repeat(shard, 8) * 2 + q
    fills, lies = [], []
    for ids, names in ((slots_one, f * 4 + h), (slots_two, h * 32 + f)):
        same = ids.reshape(1, 64) == names.reshape(128, 1)
        entry = jnp.arange(64, dtype=jnp.int32).reshape(1, 64)
        fills.append(64 + jnp.sum(jnp.where(same, entry - 64, 0), axis=1))
        lies.append(128 + jnp.sum(jnp.where(same, place.reshape(128, 1) - 128, 0), axis=0))
    return jnp.concatenate(fills + lies).astype(jnp.int32)


def body(inputs, grad_out, blocks_one, slots_one, blocks_two, slots_two):
    tab = index_tables(slots_one, slots_two)
    w1 = blocks_one.reshape(64, 128, 128)
    w2 = blocks_two.reshape(64, 128, 128)
    vmem = pl.BlockSpec(memory_space=pltpu.VMEM)
    hbm = pl.BlockSpec(memory_space=pl.ANY)
    shapes = lambda *dims, kind=F32: pltpu.VMEM(dims, kind)
    half = functools.partial(shapes, kind=BF16)
    gx, g1, g2 = pl.pallas_call(
        kernel,
        name="ffn_backward",
        out_shape=(
            jax.ShapeDtypeStruct((256, 256), F32),
            jax.ShapeDtypeStruct((4, 128, 128), F32),
            jax.ShapeDtypeStruct((4, 128, 128), F32),
        ),
        in_specs=[pl.BlockSpec(memory_space=pltpu.SMEM), vmem, vmem, hbm, hbm],
        out_specs=(vmem, vmem, vmem),
        scratch_shapes=[
            shapes(65, 128, 128), shapes(65, 128, 128),
            shapes(16, 256, 256), shapes(16, 256, 256),
            half(16, 256, 512), half(16, 256, 512),
            half(512, 256), half(512, 256),
            shapes(129, 128, 128),
            half(256, 256), half(256, 256),
            shapes(256, 512), shapes(256, 512), shapes(256, 512),
            half(512, 256), half(512, 256), half(512, 256), half(512, 256),
            half(256, 512), half(256, 512),
            shapes(16, 256, 256), shapes(17, 256, 256),
            shapes(2, 2, 16, 128, 128), shapes(2, 2, 2, 6, 128, 128), shapes(2, 4, 128, 128),
            pltpu.SemaphoreType.DMA((N_COPIES,)),
            pltpu.SemaphoreType.DMA((N_COPIES,)),
            pltpu.SemaphoreType.DMA((2,)),
        ],
        compiler_params=pltpu.CompilerParams(
            collective_id=0, has_side_effects=True, vmem_limit_bytes=66_000_000
        ),
    )(tab, inputs, grad_out, w1, w2)
    factor = 1.0 / math.sqrt(inputs.shape[0] * lax.axis_size("tok"))
    grad_one = (jnp.swapaxes(g1, 1, 2) * factor).reshape(1, 1, 4, 128, 128)
    grad_two = (g2 * factor).reshape(1, 1, 4, 128, 128)
    return gx, grad_one, grad_two


def solution(mesh):
    in_specs = (
        P("tok", "ch"),
        P("tok", "ch"),
        P(None, "ch", None, None, None),
        P(None, "ch", None),
        P(None, "ch", None, None, None),
        P(None, "ch", None),
    )
    out_specs = (P("tok", "ch"), P("tok", "ch", None, None, None), P("tok", "ch", None, None, None))
    return jax.shard_map(body, mesh=mesh, in_specs=in_specs, out_specs=out_specs, check_vma=False)
```

time: 449 us -> 136 us (0.30); the launches traced: 441 us -> 136 us
  waiting for transfers between devices: 131 us -> 0 us
  Pallas kernels: 0 us -> 127 us
  local copies, waits for them, and re-layouts: 121 us -> 4.36 us
  blocking collectives: 102 us -> 0 us
  matrix products: 58.1 us -> 0 us
  between operations: 14.6 us -> 0.72 us
  other arithmetic: 14.2 us -> 4.22 us
    all_gather x1 -> x0, waiting for transfers between devices: 131 us -> none  [side_by_side(): lax.all_gather(both, axis, axis=dim, tiled=True)]
    pallas_call x0 -> x1, Pallas kernels: none -> 127 us  [body(): pl.pallas_call(kernel, name='ffn_backward', out_shape=(jax.ShapeDtypeStru...]
    all_to_all x1 -> x0, blocking collectives: 102 us -> none  [summed_on_arrival(): lax.all_to_all(in_blocks(value, dim, peers), axis, 0, 0, tiled=True)]
    dot_general x5 -> x0, matrix products: 58.1 us -> none  [the longest x1 15.2 us: body(): grad_act = lax.dot_general(dy_full, dense_two, OUTER, precision=HIGH)]
    reshape x6 -> x0, local copies, waits for them, and re-layouts: 37.5 us -> none  [the longest x3 25.8 us: dense_to_table(): dense.reshape(first_dim, block_size, second_dim, block_size)]
    dot_general x2 -> x0, local copies, waits for them, and re-layouts: 24.9 us -> none  [body(): lax.dot_general(dense_one, grad_pre, OUTER, precision=HIGH)]
    scatter x2 -> x0, local copies, waits for them, and re-layouts: 23.3 us -> none  [rebuild(): filled = empty.at[flat_ids].set(flat_blocks, mode='drop')]
    gather x2 -> x0, local copies, waits for them, and re-layouts: 12.3 us -> none  [the longest x1 6.15 us: body(): pack_two = jnp.take(table_two, ids_two, axis=0, mode='fill', fill_value=0.0)]
  transfers between devices with their start and end apart: 2 -> 0, of which waited for: 1 -> 0; matrix products, arithmetic and copies ran while one was open for 21% -> 0% of each run, Pallas kernels for 0% -> 0%
where the time goes in v1:
time: 136 us
  Pallas kernels  127 us (93%)
  local copies, waits for them, and re-layouts  4.36 us (3%)
  other arithmetic  4.22 us (3%)
    pallas_call x1, Pallas kernels, body(): pl.pallas_call(kernel, name='ffn_backward', out_shape=(jax.ShapeDtypeStru...  127 us
    unnamed x4, local copies, waits for them, and re-layouts  4.03 us

profile of v1, /device:TPU:1, one launch (start us, length us, event | category | flops | bytes accessed | tf_op | source)
XLA Modules:
  0.0 136.0 jit_solution(312104209789370925)
XLA Ops:
  0.6 0.7 fusion.8
  1.4 0.1 broadcast_in_dim.47
  1.4 0.1 mul.49
  1.5 0.8 copy.17
  2.3 0.1 eq.40
  2.4 0.8 copy.18
  3.2 0.1 eq.45
  3.2 0.2 fusion.2
  3.5 0.7 pad_add_fusion.tab
  4.1 126.7 %ffn_backward.1 = (f32[256,256]{1,0:T(8,128)}, f32[4,128,128]{2,1,0:T(8,128)}, f32[4,128,128]{2,1,0:T(8,128)}) custom-call(s32[384]{0:T(512)} %pad_add_fusion.tab, f32[256,256]{1,0:T(8,128)} %x_in.1, f32[256,256]{1,0:T(8,128)} %dy_in.1, f32[64,128,128]{2,1,0:T(8,128)} %bitcast.12, f32[64,128,128]{2,1,0:T(8,128)} %bitcast.13), custom_call_target="tpu_custom_call" | custom-call | tf_op jit(solution)/shard_map/ffn_backward/pallas_call | solution.py:438
  130.9 1.0 multiply_bitcast_fusion.1
  131.8 0.8 copy.19
  132.7 1.7 %multiply_bitcast_fusion = f32[1,1,4,128,128]{4,3,2,1,0:T(8,128)} fusion(f32[4,128,128]{2,1,0:T(8,128)} %get-tuple-element.8), kind=kLoop, calls=%fused_computation | loop fusion | flops 65536 | bytes 524288 | tf_op jit(solution)/shard_map/reshape | solution.py:470
  134.4 1.7 %copy.21 = f32[256,256]{1,0:T(8,128)} copy(f32[256,256]{1,0:T(8,128)} %get-tuple-element.33) | data formatting | bytes 524288
  (6 shorter events, 0.0 us)

commit v2 on v1

v2 whole, which is shorter than its diff:
```python
import functools
import math

import jax
import jax.numpy as jnp
from jax import lax
from jax.experimental import pallas as pl
from jax.experimental.pallas import tpu as pltpu
from jax.sharding import PartitionSpec as P

F32 = jnp.float32
BF16 = jnp.bfloat16
MESH = pl.DeviceIdType.MESH
NZ, NXL, NXH, NY = 8, 2, 2, 4

SLOTS = [
    (0, 0),
    (0, -1), (0, 1), (1, 0),
    (0, -2), (0, 2), (1, 1),
    (0, -3), (0, 3), (1, -1),
    (0, 4), (1, -2), (1, 2),
    (1, -3), (1, 3), (1, 4),
]
SLOT = {key: at for at, key in enumerate(SLOTS)}
SLOT[(0, -4)] = SLOT[(0, 4)]
SLOT[(1, -4)] = SLOT[(1, 4)]
NT = (((1,), (1,)), ((), ()))
NN = (((1,), (0,)), ((), ()))

N_COPIES = 60 + 30 + 22


def dot(a, b, dims):
    return lax.dot_general(a, b, dims, preferred_element_type=F32)


def split(v):
    high = v.astype(BF16)
    return high, (v - high.astype(F32)).astype(BF16)


def kernel(
    ids1, ids2, x_in, dy_in, w1_hbm, w2_hbm,
    gx_out, g1_out, g2_out,
    raw1, raw2, xg, dyg, w1h, w1l, w2h, w2l, table,
    sh, sl, pre, ga, slope, act_th, act_tl, gp_th, gp_tl, gph, gpl,
    gx, rs_buf, core_buf, y_buf, far_buf, fill_v, fill, slot_of,
    send_sem, recv_sem, local_sem,
):
    t = lax.axis_index("tok")
    c = lax.axis_index("ch")
    core = lax.rem(t, 2)
    y = lax.rem(lax.div(t, 2), NY)
    xh = lax.div(t, 2 * NY)
    xl = lax.rem(c, 2)
    z = lax.div(c, 2)

    def at_z(step):
        return (t, lax.rem(z + step, NZ) * 2 + xl)

    def at_y(step):
        return ((xh * NY + lax.rem(y + step, NY)) * 2 + core, c)

    zp, zm = at_z(1), at_z(NZ - 1)
    yp, ym = at_y(1), at_y(NY - 1)
    xp = (t, z * 2 + (1 - xl))
    cp = ((xh * NY + y) * 2 + (1 - core), c)
    hp = (((1 - xh) * NY + y) * 2 + core, c)

    fetches = [
        pltpu.make_async_copy(src, dst, local_sem.at[at])
        for at, (src, dst) in enumerate(
            (
                (x_in, xg.at[0]),
                (w1_hbm, raw1.at[pl.ds(0, 64)]),
                (dy_in, dyg.at[0]),
                (w2_hbm, raw2.at[pl.ds(0, 64)]),
            )
        )
    ]

    barrier = pltpu.get_barrier_semaphore()
    for peer in (zp, zm, xp, yp, ym, cp, hp):
        pl.semaphore_signal(barrier, inc=1, device_id=peer, device_id_type=MESH)
    for fetch in fetches:
        fetch.start()
    pl.semaphore_wait(barrier, 7)

    copies = []

    def send(src, dst, peer):
        at = len(copies)
        copy = pltpu.make_async_remote_copy(
            src_ref=src, dst_ref=dst, send_sem=send_sem.at[at], recv_sem=recv_sem.at[at],
            device_id=peer, device_id_type=MESH,
        )
        copy.start()
        copies.append(copy)
        return copy

    rows = {"a": pl.ds(0, 128), "b": pl.ds(128, 128)}
    arrivals = {}

    def forward(phase, source, col, dz, half, link):
        peer = {"+": zp, "-": zm, "x": xp}[link]
        to = {"+": (col, dz - 1), "-": (col, dz + 1), "x": (1 - col, dz)}[link]
        buf = xg if phase == 0 else dyg
        src = source if (col, dz) == (0, 0) else buf.at[SLOT[(col, dz)]]
        copy = send(src.at[rows[half]], buf.at[SLOT[to], rows[half]], peer)
        arrivals[(phase, SLOT[to], half)] = copy

    def arrive(phase, key, halves="ab"):
        for half in halves:
            arrivals[(phase, SLOT[key], half)].wait_recv()

    def open_phase(phase, source):
        for one, two in ("ab", "ba"):
            forward(phase, source, 0, 0, one, "+")
            forward(phase, source, 0, 0, two, "-")
            forward(phase, source, 0, 0, one, "x")

    def gather(phase, source, take, then):
        def hand_on(col, dz, half, links):
            arrive(phase, (col, dz), half)
            for link in links:
                forward(phase, source, col, dz, half, link)

        for one, two in ("ab", "ba"):
            hand_on(0, -1, one, "+")
            hand_on(0, 1, two, "-x")
        forward(phase, source, 0, -1, "a", "x")
        forward(phase, source, 0, -1, "b", "x")
        run(take, 1, 3)
        arrive(phase, (1, 0))
        run(take, 3, 4)
        for one, two in ("ab", "ba"):
            hand_on(0, -2, one, "+")
            hand_on(0, 2, two, "-")
        run(take, 4, 6)
        arrive(phase, (1, 1))
        run(take, 6, 7)
        hand_on(0, -3, "a", "+x")
        hand_on(0, 3, "b", "-x")
        hand_on(0, -3, "b", "x")
        hand_on(0, 3, "a", "x")
        hand_on(1, -1, "a", "+")
        hand_on(1, -1, "b", "+")
        forward(phase, source, 1, 1, "b", "-")
        forward(phase, source, 1, 1, "a", "-")
        run(take, 7, 10)
        hand_on(1, -3, "a", "+")
        arrive(phase, (0, 4))
        run(take, 10, 11)
        hand_on(1, 3, "b", "-")
        then()
        arrive(phase, (1, -2))
        arrive(phase, (1, 2))
        run(take, 11, 13)
        arrive(phase, (1, -3), "b")
        run(take, 13, 14)
        arrive(phase, (1, 3), "a")
        arrive(phase, (1, 4))
        run(take, 14, 16)

    def take_x(s, carry):
        for q in range(2):
            for h in range(4):
                high, low = split(raw1[fill[0, s * 8 + q * 4 + h]])
                w1h[s, pl.ds(q * 128, 128), pl.ds(h * 128, 128)] = high
                w1l[s, pl.ds(q * 128, 128), pl.ds(h * 128, 128)] = low
        high, low = split(xg[s])
        sh[...] = high
        sl[...] = low
        pre[...] += (
            dot(sh[...], w1h[s], NN) + dot(sh[...], w1l[s], NN) + dot(sl[...], w1h[s], NN)
        )
        return carry

    def to_table(s, th, tl):
        full = dot(th[...], sh[...], NN) + dot(th[...], sl[...], NN) + dot(tl[...], sh[...], NN)
        for q in range(2):
            for h in range(4):
                table[s * 8 + q * 4 + h] = full[h * 128 : h * 128 + 128, q * 128 : q * 128 + 128]

    def take_dy(s, carry):
        for q in range(2):
            for h in range(4):
                high, low = split(raw2[fill[1, s * 8 + q * 4 + h]])
                w2h[pl.ds(h * 128, 128), pl.ds(q * 128, 128)] = high
                w2l[pl.ds(h * 128, 128), pl.ds(q * 128, 128)] = low
        high, low = split(dyg[s])
        sh[...] = high
        sl[...] = low
        ga[...] += (
            dot(sh[...], w2h[...], NT) + dot(sh[...], w2l[...], NT) + dot(sl[...], w2h[...], NT)
        )
        to_table(s, act_th, act_tl)
        return carry

    def take_w1(s, carry):
        high, low = split(xg[s])
        sh[...] = high
        sl[...] = low
        to_table(s, gp_th, gp_tl)
        return carry

    def grad_x(s, carry):
        gx[s] = dot(gph[...], w1h[s], NT) + dot(gph[...], w1l[s], NT) + dot(gpl[...], w1h[s], NT)
        return carry

    def run(body, first, last):
        lax.fori_loop(first, last, body, 0)

    def transposed(value, r, th, tl):
        high, low = split(value.T)
        th[:, r] = high
        tl[:, r] = low

    def fill_tables():
        lane = lax.broadcasted_iota(jnp.int32, (1, 128), 1)
        place = lax.div(lane, 8)
        shard = jnp.zeros_like(lane)
        for s, (col, dz) in enumerate(SLOTS):
            its = lax.rem(z + (dz + NZ), NZ) * 2 + xl + col - 2 * xl * col
            shard = jnp.where(place == s, its, shard)
            slot_of[col * NZ + (dz + NZ) % NZ] = jnp.int32(s)
        f = shard * 2 + lax.rem(lax.div(lane, 4), 2)
        h = lax.rem(lane, 4)
        one, two = f * 4 + h, h * 32 + f

        def owner(o, carry):
            a, b = carry
            for e in range(4):
                entry = o * 4 + e
                a = jnp.where(one == ids1[e, o], entry, a)
                b = jnp.where(two == ids2[e, o], entry, b)
            return a, b

        empty = jnp.full((1, 128), 64, jnp.int32)
        a, b = lax.fori_loop(0, 16, owner, (empty, empty))
        fill_v[0:1, :] = a
        fill_v[1:2, :] = b
        to_smem = pltpu.make_async_copy(fill_v, fill, local_sem.at[4])
        to_smem.start()
        to_smem.wait()

    open_phase(0, x_in)
    fill_tables()
    pre[...] = jnp.zeros_like(pre)
    ga[...] = jnp.zeros_like(ga)
    zero = jnp.zeros((128, 128), F32)
    raw1[64] = zero
    raw2[64] = zero
    table[128] = zero
    for fetch in fetches:
        fetch.wait()
    run(take_x, 0, 1)
    gather(0, x_in, take_x, lambda: open_phase(1, dy_in))
    for part in range(2):
        r = pl.ds(part * 128, 128)
        p = pre[r, :]
        cdf = 0.5 * (1.0 + lax.erf(p * (1.0 / math.sqrt(2.0))))
        pdf = jnp.exp(-0.5 * p * p) * (1.0 / math.sqrt(2.0 * math.pi))
        slope[r, :] = cdf + p * pdf
        transposed(p * cdf, r, act_th, act_tl)
    run(take_dy, 0, 1)
    gather(1, dy_in, take_dy, lambda: None)

    def lies(w, o, e):
        if w == 0:
            name = ids1[e, o]
            f, h = lax.div(name, 4), lax.rem(name, 4)
        else:
            name = ids2[e, o]
            f, h = lax.rem(name, 32), lax.div(name, 32)
        shard, q = lax.div(f, 2), lax.rem(f, 2)
        dz = lax.rem(lax.div(shard, 2) + (NZ - z), NZ)
        xs = lax.rem(shard, 2)
        slot = slot_of[(xs + xl - 2 * xs * xl) * NZ + dz]
        return jnp.where(name < 128, slot * 8 + q * 4 + h, 128)

    def pack(w, raw, rxh):
        def one(i, carry):
            rc = lax.div(i, NY)
            ry = lax.rem(i, NY)
            owner_y = lax.rem(y + ry, NY)
            owner_x = xh + rxh - 2 * xh * rxh
            owner_c = core + rc - 2 * core * rc
            owner = (owner_x * NY + owner_y) * 2 + owner_c
            for e in range(4):
                raw[((rc * 2 + rxh) * NY + ry) * 4 + e] = table[lies(w, owner, e)]
            return carry

        lax.fori_loop(0, 2 * NY, one, 0)

    def mine(raw, rxh, ry, first, count):
        return raw.at[pl.ds((rxh * NY + ry) * 4 + first, count)]

    def swap_cores(w, raw, rxh):
        return send(raw.at[pl.ds((2 + rxh) * 16, 16)], core_buf.at[w, rxh], cp)

    def add_core(copy, w, raw, rxh):
        copy.wait_recv()
        raw[pl.ds(rxh * 16, 16)] = raw[pl.ds(rxh * 16, 16)] + core_buf[w, rxh]

    def y_far(w, raw, rxh):
        return (
            send(mine(raw, rxh, 2, 0, 2), y_buf.at[w, rxh, 0, pl.ds(0, 2)], yp),
            send(mine(raw, rxh, 2, 2, 2), y_buf.at[w, rxh, 1, pl.ds(0, 2)], ym),
        )

    def y_near(pair, w, raw, rxh):
        at = (rxh * NY + 1) * 4
        pair[0].wait_recv()
        raw[pl.ds(at, 2)] = raw[pl.ds(at, 2)] + y_buf[w, rxh, 0, pl.ds(0, 2)]
        one = send(mine(raw, rxh, 1, 0, 4), y_buf.at[w, rxh, 0, pl.ds(2, 4)], yp)
        at = (rxh * NY + 3) * 4 + 2
        pair[1].wait_recv()
        raw[pl.ds(at, 2)] = raw[pl.ds(at, 2)] + y_buf[w, rxh, 1, pl.ds(0, 2)]
        two = send(mine(raw, rxh, 3, 0, 4), y_buf.at[w, rxh, 1, pl.ds(2, 4)], ym)
        return one, two

    def y_home(pair, w, raw, rxh):
        at = rxh * NY * 4
        pair[0].wait_recv()
        pair[1].wait_recv()
        raw[pl.ds(at, 4)] = (
            raw[pl.ds(at, 4)] + y_buf[w, rxh, 0, pl.ds(2, 4)] + y_buf[w, rxh, 1, pl.ds(2, 4)]
        )

    def far(w, raw):
        return send(mine(raw, 1, 0, 0, 4), far_buf.at[w], hp)

    inbound = {}

    def rs_send(col, dz, half, link):
        peer = {"+": zp, "-": zm, "x": xp}[link]
        to = {"+": (col, dz - 1), "-": (col, dz + 1), "x": (1 - col, dz)}[link]
        at = len(inbound)
        copy = send(gx.at[SLOT[(col, dz)], rows[half]], rs_buf.at[at], peer)
        inbound[(col, dz, half)] = (copy, at, SLOT[to])

    def rs_add(col, dz, half):
        copy, at, slot = inbound[(col, dz, half)]
        copy.wait_recv()
        gx[slot, rows[half]] = gx[slot, rows[half]] + rs_buf[at]

    pack(1, raw2, 1)
    core_21 = swap_cores(1, raw2, 1)
    pack(1, raw2, 0)
    core_20 = swap_cores(1, raw2, 0)

    for part in range(2):
        r = pl.ds(part * 128, 128)
        grad_pre = ga[r, :] * slope[r, :]
        high, low = split(grad_pre)
        gph[r, :] = high
        gpl[r, :] = low
        transposed(grad_pre, r, gp_th, gp_tl)

    run(grad_x, 15, 16)
    rs_send(1, 4, "a", "+")
    rs_send(1, -4, "b", "-")
    run(grad_x, 13, 15)
    rs_send(1, 3, "b", "+")
    rs_send(1, -3, "a", "-")
    run(take_w1, 0, 3)
    add_core(core_21, 1, raw2, 1)
    far_21 = y_far(1, raw2, 1)
    add_core(core_20, 1, raw2, 0)
    far_20 = y_far(1, raw2, 0)
    run(take_w1, 3, 7)
    rs_add(1, 4, "a")
    rs_send(1, 3, "a", "+")
    rs_add(1, -4, "b")
    rs_send(1, -3, "b", "-")
    run(grad_x, 11, 13)
    run(grad_x, 3, 4)
    rs_send(1, 0, "a", "x")
    rs_send(1, 0, "b", "x")
    run(take_w1, 7, 10)
    rs_add(1, 3, "b")
    rs_send(1, 2, "b", "+")
    rs_add(1, -3, "a")
    rs_send(1, -2, "a", "-")
    near_21 = y_near(far_21, 1, raw2, 1)
    run(take_w1, 10, 16)
    pack(0, raw1, 1)
    core_11 = swap_cores(0, raw1, 1)
    pack(0, raw1, 0)
    core_10 = swap_cores(0, raw1, 0)
    rs_add(1, 3, "a")
    rs_send(1, 2, "a", "+")
    rs_add(1, -3, "b")
    rs_send(1, -2, "b", "-")
    run(grad_x, 6, 11)
    rs_send(0, 4, "a", "+")
    rs_send(0, -4, "b", "-")
    rs_send(0, 3, "b", "+")
    rs_send(0, -3, "a", "-")
    add_core(core_11, 0, raw1, 1)
    far_11 = y_far(0, raw1, 1)
    add_core(core_10, 0, raw1, 0)
    far_10 = y_far(0, raw1, 0)
    rs_add(1, 2, "b")
    rs_send(1, 1, "b", "x")
    rs_add(1, -2, "a")
    rs_send(1, -1, "a", "x")
    run(grad_x, 0, 3)
    run(grad_x, 4, 6)
    y_home(near_21, 1, raw2, 1)
    far_2 = far(1, raw2)
    rs_add(1, 2, "a")
    rs_send(1, 1, "a", "x")
    rs_add(1, -2, "b")
    rs_send(1, -1, "b", "x")
    near_11 = y_near(far_11, 0, raw1, 1)
    near_20 = y_near(far_20, 1, raw2, 0)
    rs_add(0, 4, "a")
    rs_send(0, 3, "a", "+")
    rs_add(0, -4, "b")
    rs_send(0, -3, "b", "-")
    near_10 = y_near(far_10, 0, raw1, 0)
    rs_add(1, 0, "a")
    rs_add(1, 0, "b")
    rs_add(0, 3, "b")
    rs_send(0, 2, "b", "+")
    rs_add(0, -3, "a")
    rs_send(0, -2, "a", "-")
    rs_add(0, 3, "a")
    rs_send(0, 2, "a", "+")
    rs_add(0, -3, "b")
    rs_send(0, -2, "b", "-")
    y_home(near_11, 0, raw1, 1)
    far_1 = far(0, raw1)
    rs_add(1, 1, "b")
    rs_add(0, 2, "b")
    rs_send(0, 1, "b", "+")
    rs_add(1, -1, "a")
    rs_add(0, -2, "a")
    rs_send(0, -1, "a", "-")
    rs_add(1, 1, "a")
    rs_add(0, 2, "a")
    rs_send(0, 1, "a", "+")
    rs_add(1, -1, "b")
    rs_add(0, -2, "b")
    rs_send(0, -1, "b", "-")
    y_home(near_20, 1, raw2, 0)
    far_2.wait_recv()
    g2_out[...] = raw2[pl.ds(0, 4)] + far_buf[1]
    rs_add(0, 1, "b")
    rs_add(0, -1, "a")
    rs_add(0, 1, "a")
    rs_add(0, -1, "b")
    gx_out[...] = gx[0]
    y_home(near_10, 0, raw1, 0)
    far_1.wait_recv()
    g1_out[...] = raw1[pl.ds(0, 4)] + far_buf[0]
    for copy in copies:
        copy.wait_send()
    assert len(copies) == N_COPIES


def finish(factor, gx_in, g1_in, g2_in, gx_out, g1_out, g2_out):
    gx_out[...] = gx_in[...]
    for e in range(4):
        g1_out[e] = g1_in[e].T * factor
        g2_out[e] = g2_in[e] * factor


def body(inputs, grad_out, blocks_one, slots_one, blocks_two, slots_two):
    w1 = blocks_one.reshape(64, 128, 128)
    w2 = blocks_two.reshape(64, 128, 128)
    vmem = pl.BlockSpec(memory_space=pltpu.VMEM)
    hbm = pl.BlockSpec(memory_space=pl.ANY)
    smem = pl.BlockSpec(memory_space=pltpu.SMEM)
    ids = lambda slots: slots.transpose(1, 2, 0).reshape(4, 16)
    results = (
        jax.ShapeDtypeStruct((256, 256), F32),
        jax.ShapeDtypeStruct((4, 128, 128), F32),
        jax.ShapeDtypeStruct((4, 128, 128), F32),
    )
    shapes = lambda *dims, kind=F32: pltpu.VMEM(dims, kind)
    half = functools.partial(shapes, kind=BF16)
    gx, g1, g2 = pl.pallas_call(
        kernel,
        name="ffn_backward",
        out_shape=results,
        in_specs=[smem, smem, hbm, hbm, hbm, hbm],
        out_specs=(vmem, vmem, vmem),
        scratch_shapes=[
            shapes(65, 128, 128), shapes(65, 128, 128),
            shapes(16, 256, 256), shapes(16, 256, 256),
            half(16, 256, 512), half(16, 256, 512),
            half(512, 256), half(512, 256),
            shapes(129, 128, 128),
            half(256, 256), half(256, 256),
            shapes(256, 512), shapes(256, 512), shapes(256, 512),
            half(512, 256), half(512, 256), half(512, 256), half(512, 256),
            half(256, 512), half(256, 512),
            shapes(16, 256, 256), shapes(30, 128, 256),
            shapes(2, 2, 16, 128, 128), shapes(2, 2, 2, 6, 128, 128), shapes(2, 4, 128, 128),
            shapes(2, 128, kind=jnp.int32), pltpu.SMEM((2, 128), jnp.int32), pltpu.SMEM((16,), jnp.int32),
            pltpu.SemaphoreType.DMA((N_COPIES,)),
            pltpu.SemaphoreType.DMA((N_COPIES,)),
            pltpu.SemaphoreType.DMA((5,)),
        ],
        compiler_params=pltpu.CompilerParams(
            collective_id=0, has_side_effects=True, vmem_limit_bytes=66_000_000
        ),
    )(ids(slots_one), ids(slots_two), inputs, grad_out, w1, w2)
    factor = 1.0 / math.sqrt(inputs.shape[0] * lax.axis_size("tok"))
    gx, g1, g2 = pl.pallas_call(
        functools.partial(finish, factor),
        name="ffn_finish",
        out_shape=results,
        in_specs=[vmem] * 3,
        out_specs=(vmem,) * 3,
    )(gx, g1, g2)
    return gx, g1.reshape(1, 1, 4, 128, 128), g2.reshape(1, 1, 4, 128, 128)


def solution(mesh):
    in_specs = (
        P("tok", "ch"),
        P("tok", "ch"),
        P(None, "ch", None, None, None),
        P(None, "ch", None),
        P(None, "ch", None, None, None),
        P(None, "ch", None),
    )
    out_specs = (P("tok", "ch"), P("tok", "ch", None, None, None), P("tok", "ch", None, None, None))
    return jax.shard_map(body, mesh=mesh, in_specs=in_specs, out_specs=out_specs, check_vma=False)
```

time: 136 us -> 118 us (0.87)
  Pallas kernels: 127 us -> 117 us
  local copies, waits for them, and re-layouts: 4.36 us -> 0 us
  other arithmetic: 4.22 us -> 0 us
    pallas_call x1 -> x2, Pallas kernels: 127 us -> 117 us  [the longest x1 115 us: body(): pl.pallas_call(kernel, name='ffn_backward', out_shape=results, in_specs=[...]
    unnamed x4 -> x0, local copies, waits for them, and re-layouts: 4.03 us -> none
    reshape x2 -> x0, other arithmetic: 2.64 us -> none  [the longest x1 1.67 us: body(): grad_two = (g2 * factor).reshape(1, 1, 4, 128, 128)]
where the time goes in v2:
time: 118 us
  Pallas kernels  117 us (99%)
    pallas_call x1, Pallas kernels, body(): pl.pallas_call(kernel, name='ffn_backward', out_shape=results, in_specs=[...  115 us

profile of v2, /device:TPU:1, one launch (start us, length us, event | category | flops | bytes accessed | tf_op | source)
XLA Modules:
  0.0 117.7 jit_solution(17921408815373020012)
XLA Ops:
  0.6 115.0 %ffn_backward.1 = (f32[256,256]{1,0:T(8,128)}, f32[4,128,128]{2,1,0:T(8,128)}, f32[4,128,128]{2,1,0:T(8,128)}) custom-call(s32[4,16]{1,0:T(4,128)} %bitcast.12, s32[4,16]{1,0:T(4,128)} %bitcast.13, f32[256,256]{1,0:T(8,128)} %x_in.1, f32[256,256]{1,0:T(8,128)} %dy_in.1, f32[64,128,128]{2,1,0:T(8,128)} %bitcast.10, f32[64,128,128]{2,1,0:T(8,128)} %bitcast.11), custom_call_target="tpu_custom_call" | custom-call | tf_op jit(solution)/shard_map/ffn_backward/pallas_call | solution.py:485
  115.7 2.1 %ffn_finish.1 = (f32[256,256]{1,0:T(8,128)}, f32[4,128,128]{2,1,0:T(8,128)}, f32[4,128,128]{2,1,0:T(8,128)}) custom-call(f32[256,256]{1,0:T(8,128)} %get-tuple-element.9.gx_in, f32[4,128,128]{2,1,0:T(8,128)} %get-tuple-element.10.g1_in, f32[4,128,128]{2,1,0:T(8,128)} %get-tuple-element.11.g2_in), custom_call_target="tpu_custom_call" | custom-call | tf_op jit(solution)/shard_map/ffn_finish/pallas_call | solution.py:513

commit v3 on v2

--- a/solution.py
+++ b/solution.py
@@ -27,7 +27,7 @@
 NT = (((1,), (1,)), ((), ()))
 NN = (((1,), (0,)), ((), ()))
 
-N_COPIES = 60 + 30 + 22
+N_COPIES = 60 + 30 + 30
 
 
 def dot(a, b, dims):
@@ -40,11 +40,11 @@
 
 
 def kernel(
-    ids1, ids2, x_in, dy_in, w1_hbm, w2_hbm,
+    ids1_in, ids2_in, x_in, dy_in, w1_hbm, w2_hbm,
     gx_out, g1_out, g2_out,
-    raw1, raw2, xg, dyg, w1h, w1l, w2h, w2l, table,
+    raw1, raw2, xg, dyg, w1h, w1l, w2h, w2l, last_h, last_l, table,
     sh, sl, pre, ga, slope, act_th, act_tl, gp_th, gp_tl, gph, gpl,
-    gx, rs_buf, core_buf, y_buf, far_buf, fill_v, fill, slot_of,
+    gx, rs_buf, core_buf, y_buf, far_buf, fill_v, fill, slot_of, ids1, ids2, where1, where2,
     send_sem, recv_sem, local_sem,
 ):
     t = lax.axis_index("tok")
@@ -71,6 +71,8 @@
         pltpu.make_async_copy(src, dst, local_sem.at[at])
         for at, (src, dst) in enumerate(
             (
+                (ids1_in, ids1),
+                (ids2_in, ids2),
                 (x_in, xg.at[0]),
                 (w1_hbm, raw1.at[pl.ds(0, 64)]),
                 (dy_in, dyg.at[0]),
@@ -87,11 +89,24 @@
     pl.semaphore_wait(barrier, 7)
 
     copies = []
-
-    def send(src, dst, peer):
+    sent = {
+        0: xg.at[pl.ds(0, 15)], 1: dyg.at[pl.ds(0, 15)], 2: rs_buf,
+        3: core_buf.at[0], 4: core_buf.at[1], 5: y_buf.at[0], 6: y_buf.at[1],
+        7: far_buf.at[0], 8: far_buf.at[1],
+    }
+
+    def all_sent(group):
+        whole = sent[group]
+        pltpu.make_async_remote_copy(
+            src_ref=whole, dst_ref=whole, send_sem=send_sem.at[group], recv_sem=recv_sem.at[0],
+            device_id=zp, device_id_type=MESH,
+        ).wait_send()
+
+
+    def send(src, dst, peer, group):
         at = len(copies)
         copy = pltpu.make_async_remote_copy(
-            src_ref=src, dst_ref=dst, send_sem=send_sem.at[at], recv_sem=recv_sem.at[at],
+            src_ref=src, dst_ref=dst, send_sem=send_sem.at[group], recv_sem=recv_sem.at[at],
             device_id=peer, device_id_type=MESH,
         )
         copy.start()
@@ -106,7 +121,7 @@
         to = {"+": (col, dz - 1), "-": (col, dz + 1), "x": (1 - col, dz)}[link]
         buf = xg if phase == 0 else dyg
         src = source if (col, dz) == (0, 0) else buf.at[SLOT[(col, dz)]]
-        copy = send(src.at[rows[half]], buf.at[SLOT[to], rows[half]], peer)
+        copy = send(src.at[rows[half]], buf.at[SLOT[to], rows[half]], peer, phase)
         arrivals[(phase, SLOT[to], half)] = copy
 
     def arrive(phase, key, halves="ab"):
@@ -119,7 +134,7 @@
             forward(phase, source, 0, 0, two, "-")
             forward(phase, source, 0, 0, one, "x")
 
-    def gather(phase, source, take, then):
+    def gather(phase, source, take, take_last, then):
         def hand_on(col, dz, half, links):
             arrive(phase, (col, dz), half)
             for link in links:
@@ -160,7 +175,7 @@
         run(take, 13, 14)
         arrive(phase, (1, 3), "a")
         arrive(phase, (1, 4))
-        run(take, 14, 16)
+        run(take_last, 14, 16)
 
     def take_x(s, carry):
         for q in range(2):
@@ -182,18 +197,39 @@
             for h in range(4):
                 table[s * 8 + q * 4 + h] = full[h * 128 : h * 128 + 128, q * 128 : q * 128 + 128]
 
-    def take_dy(s, carry):
+    def load_dy(s):
+        high, low = split(dyg[s])
+        sh[...] = high
+        sl[...] = low
+
+    def fill_w2(s, to_h, to_l):
         for q in range(2):
             for h in range(4):
                 high, low = split(raw2[fill[1, s * 8 + q * 4 + h]])
-                w2h[pl.ds(h * 128, 128), pl.ds(q * 128, 128)] = high
-                w2l[pl.ds(h * 128, 128), pl.ds(q * 128, 128)] = low
-        high, low = split(dyg[s])
-        sh[...] = high
-        sl[...] = low
-        ga[...] += (
-            dot(sh[...], w2h[...], NT) + dot(sh[...], w2l[...], NT) + dot(sl[...], w2h[...], NT)
-        )
+                to_h[pl.ds(h * 128, 128), pl.ds(q * 128, 128)] = high
+                to_l[pl.ds(h * 128, 128), pl.ds(q * 128, 128)] = low
+
+    def add_ga(wh, wl):
+        ga[...] += dot(sh[...], wh[...], NT) + dot(sh[...], wl[...], NT) + dot(sl[...], wh[...], NT)
+
+    def take_dy(s, carry):
+        load_dy(s)
+        fill_w2(s, w2h, w2l)
+        add_ga(w2h, w2l)
+        to_table(s, act_th, act_tl)
+        return carry
+
+    def fill_last(i, carry):
+        fill_w2(14 + i, last_h.at[i], last_l.at[i])
+        return carry
+
+    def take_ga(s, carry):
+        load_dy(s)
+        add_ga(last_h.at[s - 14], last_l.at[s - 14])
+        return carry
+
+    def take_dw2(s, carry):
+        load_dy(s)
         to_table(s, act_th, act_tl)
         return carry
 
@@ -215,56 +251,6 @@
         high, low = split(value.T)
         th[:, r] = high
         tl[:, r] = low
-
-    def fill_tables():
-        lane = lax.broadcasted_iota(jnp.int32, (1, 128), 1)
-        place = lax.div(lane, 8)
-        shard = jnp.zeros_like(lane)
-        for s, (col, dz) in enumerate(SLOTS):
-            its = lax.rem(z + (dz + NZ), NZ) * 2 + xl + col - 2 * xl * col
-            shard = jnp.where(place == s, its, shard)
-            slot_of[col * NZ + (dz + NZ) % NZ] = jnp.int32(s)
-        f = shard * 2 + lax.rem(lax.div(lane, 4), 2)
-        h = lax.rem(lane, 4)
-        one, two = f * 4 + h, h * 32 + f
-
-        def owner(o, carry):
-            a, b = carry
-            for e in range(4):
-                entry = o * 4 + e
-                a = jnp.where(one == ids1[e, o], entry, a)
-                b = jnp.where(two == ids2[e, o], entry, b)
-            return a, b
-
-        empty = jnp.full((1, 128), 64, jnp.int32)
-        a, b = lax.fori_loop(0, 16, owner, (empty, empty))
-        fill_v[0:1, :] = a
-        fill_v[1:2, :] = b
-        to_smem = pltpu.make_async_copy(fill_v, fill, local_sem.at[4])
-        to_smem.start()
-        to_smem.wait()
-
-    open_phase(0, x_in)
-    fill_tables()
-    pre[...] = jnp.zeros_like(pre)
-    ga[...] = jnp.zeros_like(ga)
-    zero = jnp.zeros((128, 128), F32)
-    raw1[64] = zero
-    raw2[64] = zero
-    table[128] = zero
-    for fetch in fetches:
-        fetch.wait()
-    run(take_x, 0, 1)
-    gather(0, x_in, take_x, lambda: open_phase(1, dy_in))
-    for part in range(2):
-        r = pl.ds(part * 128, 128)
-        p = pre[r, :]
-        cdf = 0.5 * (1.0 + lax.erf(p * (1.0 / math.sqrt(2.0))))
-        pdf = jnp.exp(-0.5 * p * p) * (1.0 / math.sqrt(2.0 * math.pi))
-        slope[r, :] = cdf + p * pdf
-        transposed(p * cdf, r, act_th, act_tl)
-    run(take_dy, 0, 1)
-    gather(1, dy_in, take_dy, lambda: None)
 
     def lies(w, o, e):
         if w == 0:
@@ -279,45 +265,124 @@
         slot = slot_of[(xs + xl - 2 * xs * xl) * NZ + dz]
         return jnp.where(name < 128, slot * 8 + q * 4 + h, 128)
 
-    def pack(w, raw, rxh):
+    def fill_tables():
+        lane = lax.broadcasted_iota(jnp.int32, (1, 128), 1)
+        place = lax.div(lane, 8)
+        shard = jnp.zeros_like(lane)
+        for s, (col, dz) in enumerate(SLOTS):
+            its = lax.rem(z + (dz + NZ), NZ) * 2 + xl + col - 2 * xl * col
+            shard = jnp.where(place == s, its, shard)
+            slot_of[col * NZ + (dz + NZ) % NZ] = jnp.int32(s)
+        f = shard * 2 + lax.rem(lax.div(lane, 4), 2)
+        h = lax.rem(lane, 4)
+        one, two = f * 4 + h, h * 32 + f
+
+        def owner(o, carry):
+            a, b = carry
+            for e in range(4):
+                entry = o * 4 + e
+                a = jnp.where(one == ids1[e, o], entry, a)
+                b = jnp.where(two == ids2[e, o], entry, b)
+            return a, b
+
+        empty = jnp.full((1, 128), 64, jnp.int32)
+        a, b = lax.fori_loop(0, 16, owner, (empty, empty))
+        fill_v[0:1, :] = a
+        fill_v[1:2, :] = b
+        to_smem = pltpu.make_async_copy(fill_v, fill, local_sem.at[6])
+        to_smem.start()
+        to_smem.wait()
+
+    def find_entries():
+        def owner(o, carry):
+            for e in range(4):
+                where1[o * 4 + e] = lies(0, o, e)
+                where2[o * 4 + e] = lies(1, o, e)
+            return carry
+
+        lax.fori_loop(0, 16, owner, 0)
+
+    open_phase(0, x_in)
+    fetches[0].wait()
+    fetches[1].wait()
+    fill_tables()
+    pre[...] = jnp.zeros_like(pre)
+    ga[...] = jnp.zeros_like(ga)
+    zero = jnp.zeros((128, 128), F32)
+    raw1[64] = zero
+    raw2[64] = zero
+    table[128] = zero
+    for fetch in fetches[2:]:
+        fetch.wait()
+    run(take_x, 0, 1)
+
+    def next_phase():
+        open_phase(1, dy_in)
+        find_entries()
+
+    gather(0, x_in, take_x, take_x, next_phase)
+    for part in range(2):
+        r = pl.ds(part * 128, 128)
+        p = pre[r, :]
+        cdf = 0.5 * (1.0 + lax.erf(p * (1.0 / math.sqrt(2.0))))
+        pdf = jnp.exp(-0.5 * p * p) * (1.0 / math.sqrt(2.0 * math.pi))
+        slope[r, :] = cdf + p * pdf
+        transposed(p * cdf, r, act_th, act_tl)
+    run(take_dy, 0, 1)
+    gather(1, dy_in, take_dy, take_dw2, lambda: run(fill_last, 0, 2))
+
+    def pack(w, raw, rxh, first, last):
+        where = where2 if w else where1
+
         def one(i, carry):
-            rc = lax.div(i, NY)
-            ry = lax.rem(i, NY)
+            rc = lax.rem(i, 2)
+            ry = lax.div(i, 2)
             owner_y = lax.rem(y + ry, NY)
             owner_x = xh + rxh - 2 * xh * rxh
             owner_c = core + rc - 2 * core * rc
             owner = (owner_x * NY + owner_y) * 2 + owner_c
             for e in range(4):
-                raw[((rc * 2 + rxh) * NY + ry) * 4 + e] = table[lies(w, owner, e)]
+                raw[((rc * 2 + rxh) * NY + ry) * 4 + e] = table[where[owner * 4 + e]]
             return carry
 
-        lax.fori_loop(0, 2 * NY, one, 0)
+        lax.fori_loop(2 * first, 2 * last, one, 0)
 
     def mine(raw, rxh, ry, first, count):
         return raw.at[pl.ds((rxh * NY + ry) * 4 + first, count)]
 
-    def swap_cores(w, raw, rxh):
-        return send(raw.at[pl.ds((2 + rxh) * 16, 16)], core_buf.at[w, rxh], cp)
-
-    def add_core(copy, w, raw, rxh):
+    def swap_cores(w, raw, rxh, first, last):
+        r = pl.ds(first * 4, (last - first) * 4)
+        theirs = pl.ds(((2 + rxh) * NY + first) * 4, (last - first) * 4)
+        return send(raw.at[theirs], core_buf.at[w, rxh, r], cp, 3 + w), first, last
+
+    def add_core(swap, w, raw, rxh):
+        copy, first, last = swap
         copy.wait_recv()
-        raw[pl.ds(rxh * 16, 16)] = raw[pl.ds(rxh * 16, 16)] + core_buf[w, rxh]
+        ours = pl.ds((rxh * NY + first) * 4, (last - first) * 4)
+        raw[ours] = raw[ours] + core_buf[w, rxh, pl.ds(first * 4, (last - first) * 4)]
+
+    def swap_all(w, raw):
+        swaps = {}
+        for rxh, first, last in ((1, 2, 3), (0, 2, 3), (1, 3, 4), (1, 0, 2), (0, 3, 4), (0, 0, 2)):
+            pack(w, raw, rxh, first, last)
+            swaps[(rxh, first)] = swap_cores(w, raw, rxh, first, last)
+        return swaps
 
     def y_far(w, raw, rxh):
         return (
-            send(mine(raw, rxh, 2, 0, 2), y_buf.at[w, rxh, 0, pl.ds(0, 2)], yp),
-            send(mine(raw, rxh, 2, 2, 2), y_buf.at[w, rxh, 1, pl.ds(0, 2)], ym),
+            send(mine(raw, rxh, 2, 0, 2), y_buf.at[w, rxh, 0, pl.ds(0, 2)], yp, 5 + w),
+            send(mine(raw, rxh, 2, 2, 2), y_buf.at[w, rxh, 1, pl.ds(0, 2)], ym, 5 + w),
         )
 
     def y_near(pair, w, raw, rxh):
         at = (rxh * NY + 1) * 4
         pair[0].wait_recv()
         raw[pl.ds(at, 2)] = raw[pl.ds(at, 2)] + y_buf[w, rxh, 0, pl.ds(0, 2)]
-        one = send(mine(raw, rxh, 1, 0, 4), y_buf.at[w, rxh, 0, pl.ds(2, 4)], yp)
+        one = send(mine(raw, rxh, 1, 0, 4), y_buf.at[w, rxh, 0, pl.ds(2, 4)], yp, 5 + w)
         at = (rxh * NY + 3) * 4 + 2
         pair[1].wait_recv()
         raw[pl.ds(at, 2)] = raw[pl.ds(at, 2)] + y_buf[w, rxh, 1, pl.ds(0, 2)]
-        two = send(mine(raw, rxh, 3, 0, 4), y_buf.at[w, rxh, 1, pl.ds(2, 4)], ym)
+        two = send(mine(raw, rxh, 3, 0, 4), y_buf.at[w, rxh, 1, pl.ds(2, 4)], ym, 5 + w)
         return one, two
 
     def y_home(pair, w, raw, rxh):
@@ -329,7 +394,7 @@
         )
 
     def far(w, raw):
-        return send(mine(raw, 1, 0, 0, 4), far_buf.at[w], hp)
+        return send(mine(raw, 1, 0, 0, 4), far_buf.at[w], hp, 7 + w)
 
     inbound = {}
 
@@ -337,7 +402,7 @@
         peer = {"+": zp, "-": zm, "x": xp}[link]
         to = {"+": (col, dz - 1), "-": (col, dz + 1), "x": (1 - col, dz)}[link]
         at = len(inbound)
-        copy = send(gx.at[SLOT[(col, dz)], rows[half]], rs_buf.at[at], peer)
+        copy = send(gx.at[SLOT[(col, dz)], rows[half]], rs_buf.at[at], peer, 2)
         inbound[(col, dz, half)] = (copy, at, SLOT[to])
 
     def rs_add(col, dz, half):
@@ -345,11 +410,8 @@
         copy.wait_recv()
         gx[slot, rows[half]] = gx[slot, rows[half]] + rs_buf[at]
 
-    pack(1, raw2, 1)
-    core_21 = swap_cores(1, raw2, 1)
-    pack(1, raw2, 0)
-    core_20 = swap_cores(1, raw2, 0)
-
+    swap_2 = swap_all(1, raw2)
+    run(take_ga, 14, 16)
     for part in range(2):
         r = pl.ds(part * 128, 128)
         grad_pre = ga[r, :] * slope[r, :]
@@ -357,63 +419,68 @@
         gph[r, :] = high
         gpl[r, :] = low
         transposed(grad_pre, r, gp_th, gp_tl)
-
     run(grad_x, 15, 16)
-    rs_send(1, 4, "a", "+")
-    rs_send(1, -4, "b", "-")
+    rs_send(1, 4, "a", "x")
+    rs_send(1, 4, "b", "x")
+    add_core(swap_2[(1, 2)], 1, raw2, 1)
+    far_21 = y_far(1, raw2, 1)
     run(grad_x, 13, 15)
     rs_send(1, 3, "b", "+")
     rs_send(1, -3, "a", "-")
-    run(take_w1, 0, 3)
-    add_core(core_21, 1, raw2, 1)
-    far_21 = y_far(1, raw2, 1)
-    add_core(core_20, 1, raw2, 0)
+    rs_send(1, 3, "a", "+")
+    rs_send(1, -3, "b", "-")
+    add_core(swap_2[(0, 2)], 1, raw2, 0)
     far_20 = y_far(1, raw2, 0)
-    run(take_w1, 3, 7)
-    rs_add(1, 4, "a")
-    rs_send(1, 3, "a", "+")
-    rs_add(1, -4, "b")
-    rs_send(1, -3, "b", "-")
-    run(grad_x, 11, 13)
+    run(take_w1, 0, 5)
     run(grad_x, 3, 4)
     rs_send(1, 0, "a", "x")
     rs_send(1, 0, "b", "x")
-    run(take_w1, 7, 10)
+    add_core(swap_2[(1, 3)], 1, raw2, 1)
+    add_core(swap_2[(1, 0)], 1, raw2, 1)
+    add_core(swap_2[(0, 3)], 1, raw2, 0)
+    add_core(swap_2[(0, 0)], 1, raw2, 0)
+    run(grad_x, 11, 13)
+    run(take_w1, 5, 6)
+    near_21 = y_near(far_21, 1, raw2, 1)
     rs_add(1, 3, "b")
     rs_send(1, 2, "b", "+")
     rs_add(1, -3, "a")
     rs_send(1, -2, "a", "-")
-    near_21 = y_near(far_21, 1, raw2, 1)
-    run(take_w1, 10, 16)
-    pack(0, raw1, 1)
-    core_11 = swap_cores(0, raw1, 1)
-    pack(0, raw1, 0)
-    core_10 = swap_cores(0, raw1, 0)
+    run(take_w1, 6, 11)
     rs_add(1, 3, "a")
     rs_send(1, 2, "a", "+")
     rs_add(1, -3, "b")
     rs_send(1, -2, "b", "-")
-    run(grad_x, 6, 11)
+    run(take_w1, 11, 16)
+    swap_1 = swap_all(0, raw1)
+    run(grad_x, 10, 11)
+    rs_add(1, 4, "a")
     rs_send(0, 4, "a", "+")
+    rs_add(1, 4, "b")
     rs_send(0, -4, "b", "-")
+    run(grad_x, 6, 10)
     rs_send(0, 3, "b", "+")
     rs_send(0, -3, "a", "-")
-    add_core(core_11, 0, raw1, 1)
-    far_11 = y_far(0, raw1, 1)
-    add_core(core_10, 0, raw1, 0)
-    far_10 = y_far(0, raw1, 0)
     rs_add(1, 2, "b")
     rs_send(1, 1, "b", "x")
     rs_add(1, -2, "a")
     rs_send(1, -1, "a", "x")
-    run(grad_x, 0, 3)
-    run(grad_x, 4, 6)
-    y_home(near_21, 1, raw2, 1)
-    far_2 = far(1, raw2)
+    add_core(swap_1[(1, 2)], 0, raw1, 1)
+    far_11 = y_far(0, raw1, 1)
+    add_core(swap_1[(0, 2)], 0, raw1, 0)
+    far_10 = y_far(0, raw1, 0)
     rs_add(1, 2, "a")
     rs_send(1, 1, "a", "x")
     rs_add(1, -2, "b")
     rs_send(1, -1, "b", "x")
+    y_home(near_21, 1, raw2, 1)
+    far_2 = far(1, raw2)
+    add_core(swap_1[(1, 3)], 0, raw1, 1)
+    add_core(swap_1[(1, 0)], 0, raw1, 1)
+    add_core(swap_1[(0, 3)], 0, raw1, 0)
+    add_core(swap_1[(0, 0)], 0, raw1, 0)
+    run(grad_x, 0, 3)
+    run(grad_x, 4, 6)
     near_11 = y_near(far_11, 0, raw1, 1)
     near_20 = y_near(far_20, 1, raw2, 0)
     rs_add(0, 4, "a")
@@ -423,6 +490,8 @@
     near_10 = y_near(far_10, 0, raw1, 0)
     rs_add(1, 0, "a")
     rs_add(1, 0, "b")
+    all_sent(0)
+    all_sent(1)
     rs_add(0, 3, "b")
     rs_send(0, 2, "b", "+")
     rs_add(0, -3, "a")
@@ -447,17 +516,25 @@
     rs_send(0, -1, "b", "-")
     y_home(near_20, 1, raw2, 0)
     far_2.wait_recv()
-    g2_out[...] = raw2[pl.ds(0, 4)] + far_buf[1]
+    raw2[pl.ds(0, 4)] = raw2[pl.ds(0, 4)] + far_buf[1]
+    put_g2 = pltpu.make_async_copy(raw2.at[pl.ds(0, 4)], g2_out, local_sem.at[7])
+    put_g2.start()
     rs_add(0, 1, "b")
     rs_add(0, -1, "a")
     rs_add(0, 1, "a")
     rs_add(0, -1, "b")
-    gx_out[...] = gx[0]
+    put_gx = pltpu.make_async_copy(gx.at[0], gx_out, local_sem.at[8])
+    put_gx.start()
     y_home(near_10, 0, raw1, 0)
     far_1.wait_recv()
-    g1_out[...] = raw1[pl.ds(0, 4)] + far_buf[0]
-    for copy in copies:
-        copy.wait_send()
+    raw1[pl.ds(0, 4)] = raw1[pl.ds(0, 4)] + far_buf[0]
+    put_g1 = pltpu.make_async_copy(raw1.at[pl.ds(0, 4)], g1_out, local_sem.at[9])
+    put_g1.start()
+    for group in range(2, 9):
+        all_sent(group)
+    put_g2.wait()
+    put_gx.wait()
+    put_g1.wait()
     assert len(copies) == N_COPIES
 
 
@@ -472,8 +549,7 @@
     w1 = blocks_one.reshape(64, 128, 128)
     w2 = blocks_two.reshape(64, 128, 128)
     vmem = pl.BlockSpec(memory_space=pltpu.VMEM)
-    hbm = pl.BlockSpec(memory_space=pl.ANY)
-    smem = pl.BlockSpec(memory_space=pltpu.SMEM)
+    hbm = pl.BlockSpec(memory_space=pltpu.HBM)
     ids = lambda slots: slots.transpose(1, 2, 0).reshape(4, 16)
     results = (
         jax.ShapeDtypeStruct((256, 256), F32),
@@ -486,13 +562,13 @@
         kernel,
         name="ffn_backward",
         out_shape=results,
-        in_specs=[smem, smem, hbm, hbm, hbm, hbm],
-        out_specs=(vmem, vmem, vmem),
+        in_specs=[hbm] * 6,
+        out_specs=(hbm,) * 3,
         scratch_shapes=[
             shapes(65, 128, 128), shapes(65, 128, 128),
             shapes(16, 256, 256), shapes(16, 256, 256),
             half(16, 256, 512), half(16, 256, 512),
-            half(512, 256), half(512, 256),
+            half(512, 256), half(512, 256), half(2, 512, 256), half(2, 512, 256),
             shapes(129, 128, 128),
             half(256, 256), half(256, 256),
             shapes(256, 512), shapes(256, 512), shapes(256, 512),
@@ -501,12 +577,14 @@
             shapes(16, 256, 256), shapes(30, 128, 256),
             shapes(2, 2, 16, 128, 128), shapes(2, 2, 2, 6, 128, 128), shapes(2, 4, 128, 128),
             shapes(2, 128, kind=jnp.int32), pltpu.SMEM((2, 128), jnp.int32), pltpu.SMEM((16,), jnp.int32),
+            pltpu.SMEM((4, 16), jnp.int32), pltpu.SMEM((4, 16), jnp.int32),
+            pltpu.SMEM((64,), jnp.int32), pltpu.SMEM((64,), jnp.int32),
+            pltpu.SemaphoreType.DMA((9,)),
             pltpu.SemaphoreType.DMA((N_COPIES,)),
-            pltpu.SemaphoreType.DMA((N_COPIES,)),
-            pltpu.SemaphoreType.DMA((5,)),
+            pltpu.SemaphoreType.DMA((10,)),
         ],
         compiler_params=pltpu.CompilerParams(
-            collective_id=0, has_side_effects=True, vmem_limit_bytes=66_000_000
+            collective_id=0, has_side_effects=True, vmem_limit_bytes=60_000_000
         ),
     )(ids(slots_one), ids(slots_two), inputs, grad_out, w1, w2)
     factor = 1.0 / math.sqrt(inputs.shape[0] * lax.axis_size("tok"))

time: 118 us -> 113 us (0.958)
  Pallas kernels: 117 us -> 113 us
    pallas_call x1, Pallas kernels: 115 us -> 111 us  [body(): pl.pallas_call(kernel, name='ffn_backward', out_shape=results, in_specs=[...]
where the time goes in v3:
time: 113 us
  Pallas kernels  113 us (100%)
    pallas_call x1, Pallas kernels, body(): pl.pallas_call(kernel, name='ffn_backward', out_shape=results, in_specs=[...  111 us

profile of v3, /device:TPU:1, one launch (start us, length us, event | category | flops | bytes accessed | tf_op | source)
XLA Modules:
  0.0 113.3 jit_solution(17876377293662306778)
XLA Ops:
  0.6 110.6 %ffn_backward.1 = (f32[256,256]{1,0:T(8,128)}, f32[4,128,128]{2,1,0:T(8,128)}, f32[4,128,128]{2,1,0:T(8,128)}) custom-call(s32[4,16]{1,0:T(4,128)} %bitcast.12, s32[4,16]{1,0:T(4,128)} %bitcast.13, f32[256,256]{1,0:T(8,128)} %x_in.1, f32[256,256]{1,0:T(8,128)} %dy_in.1, f32[64,128,128]{2,1,0:T(8,128)} %bitcast.10, f32[64,128,128]{2,1,0:T(8,128)} %bitcast.11), custom_call_target="tpu_custom_call" | custom-call | tf_op jit(solution)/shard_map/ffn_backward/pallas_call | solution.py:561
  111.2 2.1 %ffn_finish.1 = (f32[256,256]{1,0:T(8,128)}, f32[4,128,128]{2,1,0:T(8,128)}, f32[4,128,128]{2,1,0:T(8,128)}) custom-call(f32[256,256]{1,0:T(8,128)} %get-tuple-element.9.gx_in, f32[4,128,128]{2,1,0:T(8,128)} %get-tuple-element.10.g1_in, f32[4,128,128]{2,1,0:T(8,128)} %get-tuple-element.11.g2_in), custom_call_target="tpu_custom_call" | custom-call | tf_op jit(solution)/shard_map/ffn_finish/pallas_call | solution.py:591

commit v4 on v3

--- a/solution.py
+++ b/solution.py
@@ -429,9 +429,10 @@
     rs_send(1, -3, "a", "-")
     rs_send(1, 3, "a", "+")
     rs_send(1, -3, "b", "-")
+    run(take_w1, 0, 3)
     add_core(swap_2[(0, 2)], 1, raw2, 0)
     far_20 = y_far(1, raw2, 0)
-    run(take_w1, 0, 5)
+    run(take_w1, 3, 5)
     run(grad_x, 3, 4)
     rs_send(1, 0, "a", "x")
     rs_send(1, 0, "b", "x")
@@ -440,24 +441,25 @@
     add_core(swap_2[(0, 3)], 1, raw2, 0)
     add_core(swap_2[(0, 0)], 1, raw2, 0)
     run(grad_x, 11, 13)
-    run(take_w1, 5, 6)
+    run(take_w1, 5, 8)
     near_21 = y_near(far_21, 1, raw2, 1)
     rs_add(1, 3, "b")
     rs_send(1, 2, "b", "+")
     rs_add(1, -3, "a")
     rs_send(1, -2, "a", "-")
-    run(take_w1, 6, 11)
+    run(take_w1, 8, 16)
+    swap_1 = swap_all(0, raw1)
     rs_add(1, 3, "a")
     rs_send(1, 2, "a", "+")
     rs_add(1, -3, "b")
     rs_send(1, -2, "b", "-")
-    run(take_w1, 11, 16)
-    swap_1 = swap_all(0, raw1)
     run(grad_x, 10, 11)
     rs_add(1, 4, "a")
     rs_send(0, 4, "a", "+")
     rs_add(1, 4, "b")
     rs_send(0, -4, "b", "-")
+    add_core(swap_1[(1, 2)], 0, raw1, 1)
+    far_11 = y_far(0, raw1, 1)
     run(grad_x, 6, 10)
     rs_send(0, 3, "b", "+")
     rs_send(0, -3, "a", "-")
@@ -465,15 +467,13 @@
     rs_send(1, 1, "b", "x")
     rs_add(1, -2, "a")
     rs_send(1, -1, "a", "x")
-    add_core(swap_1[(1, 2)], 0, raw1, 1)
-    far_11 = y_far(0, raw1, 1)
     add_core(swap_1[(0, 2)], 0, raw1, 0)
     far_10 = y_far(0, raw1, 0)
+    y_home(near_21, 1, raw2, 1)
     rs_add(1, 2, "a")
     rs_send(1, 1, "a", "x")
     rs_add(1, -2, "b")
     rs_send(1, -1, "b", "x")
-    y_home(near_21, 1, raw2, 1)
     far_2 = far(1, raw2)
     add_core(swap_1[(1, 3)], 0, raw1, 1)
     add_core(swap_1[(1, 0)], 0, raw1, 1)
@@ -481,15 +481,15 @@
     add_core(swap_1[(0, 0)], 0, raw1, 0)
     run(grad_x, 0, 3)
     run(grad_x, 4, 6)
-    near_11 = y_near(far_11, 0, raw1, 1)
-    near_20 = y_near(far_20, 1, raw2, 0)
     rs_add(0, 4, "a")
     rs_send(0, 3, "a", "+")
     rs_add(0, -4, "b")
     rs_send(0, -3, "b", "-")
-    near_10 = y_near(far_10, 0, raw1, 0)
+    near_11 = y_near(far_11, 0, raw1, 1)
+    near_20 = y_near(far_20, 1, raw2, 0)
     rs_add(1, 0, "a")
     rs_add(1, 0, "b")
+    near_10 = y_near(far_10, 0, raw1, 0)
     all_sent(0)
     all_sent(1)
     rs_add(0, 3, "b")

time: 113 us -> 114 us (level)
  no operation moved by 1% of the time
where the time goes in v4:
time: 114 us
  Pallas kernels  113 us (99%)
    pallas_call x1, Pallas kernels, body(): pl.pallas_call(kernel, name='ffn_backward', out_shape=results, in_specs=[...  111 us

profile of v4, /device:TPU:1, one launch (start us, length us, event | category | flops | bytes accessed | tf_op | source)
XLA Modules:
  0.0 114.1 jit_solution(6705305303206033226)
XLA Ops:
  0.6 111.4 %ffn_backward.1 = (f32[256,256]{1,0:T(8,128)}, f32[4,128,128]{2,1,0:T(8,128)}, f32[4,128,128]{2,1,0:T(8,128)}) custom-call(s32[4,16]{1,0:T(4,128)} %bitcast.12, s32[4,16]{1,0:T(4,128)} %bitcast.13, f32[256,256]{1,0:T(8,128)} %x_in.1, f32[256,256]{1,0:T(8,128)} %dy_in.1, f32[64,128,128]{2,1,0:T(8,128)} %bitcast.10, f32[64,128,128]{2,1,0:T(8,128)} %bitcast.11), custom_call_target="tpu_custom_call" | custom-call | tf_op jit(solution)/shard_map/ffn_backward/pallas_call | solution.py:561
  112.1 2.1 %ffn_finish.1 = (f32[256,256]{1,0:T(8,128)}, f32[4,128,128]{2,1,0:T(8,128)}, f32[4,128,128]{2,1,0:T(8,128)}) custom-call(f32[256,256]{1,0:T(8,128)} %get-tuple-element.9.gx_in, f32[4,128,128]{2,1,0:T(8,128)} %get-tuple-element.10.g1_in, f32[4,128,128]{2,1,0:T(8,128)} %get-tuple-element.11.g2_in), custom_call_target="tpu_custom_call" | custom-call | tf_op jit(solution)/shard_map/ffn_finish/pallas_call | solution.py:591

commit v5 on v4

--- a/solution.py
+++ b/solution.py
@@ -480,16 +480,14 @@
     add_core(swap_1[(0, 3)], 0, raw1, 0)
     add_core(swap_1[(0, 0)], 0, raw1, 0)
     run(grad_x, 0, 3)
+    near_11 = y_near(far_11, 0, raw1, 1)
     run(grad_x, 4, 6)
     rs_add(0, 4, "a")
     rs_send(0, 3, "a", "+")
     rs_add(0, -4, "b")
     rs_send(0, -3, "b", "-")
-    near_11 = y_near(far_11, 0, raw1, 1)
-    near_20 = y_near(far_20, 1, raw2, 0)
     rs_add(1, 0, "a")
     rs_add(1, 0, "b")
-    near_10 = y_near(far_10, 0, raw1, 0)
     all_sent(0)
     all_sent(1)
     rs_add(0, 3, "b")
@@ -500,8 +498,10 @@
     rs_send(0, 2, "a", "+")
     rs_add(0, -3, "b")
     rs_send(0, -2, "b", "-")
+    near_20 = y_near(far_20, 1, raw2, 0)
     y_home(near_11, 0, raw1, 1)
     far_1 = far(0, raw1)
+    near_10 = y_near(far_10, 0, raw1, 0)
     rs_add(1, 1, "b")
     rs_add(0, 2, "b")
     rs_send(0, 1, "b", "+")

time: 114 us -> 114 us (level)
  no operation moved by 1% of the time
where the time goes in v5:
time: 114 us
  Pallas kernels  113 us (99%)
    pallas_call x1, Pallas kernels, body(): pl.pallas_call(kernel, name='ffn_backward', out_shape=results, in_specs=[...  111 us

profile of v5, /device:TPU:1, one launch (start us, length us, event | category | flops | bytes accessed | tf_op | source)
XLA Modules:
  0.0 114.1 jit_solution(16643573033244802235)
XLA Ops:
  0.6 111.4 %ffn_backward.1 = (f32[256,256]{1,0:T(8,128)}, f32[4,128,128]{2,1,0:T(8,128)}, f32[4,128,128]{2,1,0:T(8,128)}) custom-call(s32[4,16]{1,0:T(4,128)} %bitcast.12, s32[4,16]{1,0:T(4,128)} %bitcast.13, f32[256,256]{1,0:T(8,128)} %x_in.1, f32[256,256]{1,0:T(8,128)} %dy_in.1, f32[64,128,128]{2,1,0:T(8,128)} %bitcast.10, f32[64,128,128]{2,1,0:T(8,128)} %bitcast.11), custom_call_target="tpu_custom_call" | custom-call | tf_op jit(solution)/shard_map/ffn_backward/pallas_call | solution.py:561
  112.1 2.1 %ffn_finish.1 = (f32[256,256]{1,0:T(8,128)}, f32[4,128,128]{2,1,0:T(8,128)}, f32[4,128,128]{2,1,0:T(8,128)}) custom-call(f32[256,256]{1,0:T(8,128)} %get-tuple-element.9.gx_in, f32[4,128,128]{2,1,0:T(8,128)} %get-tuple-element.10.g1_in, f32[4,128,128]{2,1,0:T(8,128)} %get-tuple-element.11.g2_in), custom_call_target="tpu_custom_call" | custom-call | tf_op jit(solution)/shard_map/ffn_finish/pallas_call | solution.py:591
